TPU v7x, 32 devices: a whole 2x2x4 slice. The times are simulated.
32 devices in a mesh: shard: 2 (over core), context: 4 (over y, x), tensor: 4 (over z).
Axes of the slice: x: 2, y: 2, z: 4, core: 2. Of those that a mesh axis runs over, the one named last changes fastest.
Arguments:
- tokens: bfloat16 [2, 4096, 1536], P('shard', 'context'), may hold values from -6 to 6
- w_query: bfloat16 [1536, 1536], P('shard', 'tensor'), may hold values from -0.15625 to 0.15625
- key_weight: bfloat16 [1536, 768], P('shard', 'tensor'), may hold values from -0.15625 to 0.15625
- value_weight: bfloat16 [1536, 768], P('shard', 'tensor'), may hold values from -0.15625 to 0.15625
- w_out: bfloat16 [1536, 1536], P('tensor', 'shard'), may hold values from -0.625 to 0.625
- w_gate: bfloat16 [1536, 4096], P('shard', 'tensor'), may hold values from -0.15625 to 0.15625
- w_up: bfloat16 [1536, 4096], P('shard', 'tensor'), may hold values from -0.15625 to 0.15625
- w_down: bfloat16 [4096, 1536], P('tensor', 'shard'), may hold values from -0.09375 to 0.09375
- gain_attn: bfloat16 [1536], P('shard'), may hold values from 0.5 to 1.5
- gain_ffn: bfloat16 [1536], P('shard'), may hold values from 0.5 to 1.5
- segments: int32 [2, 4096], P('shard'), may hold values from 0 to 8, as said below
- positions: int32 [2, 4096], P('shard'), may hold values from 0 to 2303, as said below
- cotangent: bfloat16 [2, 4096, 1536], P('shard', 'context'), may hold values from -6 to 6
Outputs:
- output: bfloat16 [2, 4096, 1536], P('shard', 'context')
- tokens_grad: bfloat16 [2, 4096, 1536], P('shard', 'context')
- w_query_grad: float32 [1536, 1536], P('shard', 'tensor')
- w_key_grad: float32 [1536, 768], P('shard', 'tensor')
- w_value_grad: float32 [1536, 768], P('shard', 'tensor')
- w_out_grad: float32 [1536, 1536], P('tensor', 'shard')
- w_gate_grad: float32 [1536, 4096], P('shard', 'tensor')
- w_up_grad: float32 [1536, 4096], P('shard', 'tensor')
- w_down_grad: float32 [4096, 1536], P('tensor', 'shard')
- gain_attn_grad: float32 [1536], P('shard')
- gain_ffn_grad: float32 [1536], P('shard')
Inputs may be any that keep to these rules, and one draw needn't show every extreme that they name: In each group, segment 0 is a prompt of 2048 tokens and segments 1 to 8 are continuations of 256 tokens each; continuation number c branches off the prompt after its first c * 256 positions. Even slots 2 i hold the prompt half and odd slots 2 i + 1 the continuation half, each half being 2048 rows indexed by i. The prompt half is made of runs of 256 rows, each run holding 256 consecutive prompt tokens in order, the order of the runs drawn; the continuation half is made of runs of 256 rows, each run one whole continuation in order, the order of the continuations drawn. A prompt token's position is its index in the prompt; a continuation's token is at 2048 plus its index in the continuation; positions rise by one along each aligned block of 256 rows of a half.
All inputs are finite; a program needn't handle non-finite values.
Results may differ from a plain program's by a relative error of at most 0.015.
Values may be sent and summed in bfloat16 or wider, within the bound.
A program may use at most 384 MiB of HBM per device.

v0:
```python
import functools
import math

import jax
import jax.numpy as jnp
import numpy as np
from jax import lax
from jax.experimental import pallas as pl
from jax.experimental.pallas import tpu as pltpu
from jax.sharding import PartitionSpec as P

HEAD_SIZE = 96
CLEN = 256


rope_base = 100000.0
norm_eps = 1e-05


def tables(positions):
    half_width = HEAD_SIZE // 2
    frequency = jnp.exp(
        jnp.arange(half_width, dtype=jnp.float32) * (-2.0 * math.log(rope_base) / HEAD_SIZE)
    )
    angles = positions.astype(jnp.float32)[:, None] * frequency[None, :]
    return (jnp.cos(angles)[:, None, :], jnp.sin(angles)[:, None, :])


def rotary_apply(heads, cosine_table, sine_values):
    half_width = HEAD_SIZE // 2
    front_half = heads[..., :half_width]
    back_half = heads[..., half_width:]
    return jnp.concatenate(
        [
            front_half * cosine_table - back_half * sine_values,
            back_half * cosine_table + front_half * sine_values,
        ],
        axis=-1,
    )


def rotate_back(heads, cosine_table, sine_values):
    half_width = HEAD_SIZE // 2
    front_half = heads[..., :half_width]
    back_half = heads[..., half_width:]
    return jnp.concatenate(
        [
            front_half * cosine_table + back_half * sine_values,
            back_half * cosine_table - front_half * sine_values,
        ],
        axis=-1,
    )


def contract_rows(left, right):
    return lax.dot_general(
        left, right, (((0,), (0,)), ((), ())), preferred_element_type=jnp.float32
    )


def contract_cols(left, right):
    return lax.dot_general(
        left, right, (((1,), (1,)), ((), ())), preferred_element_type=jnp.float32
    )


def norm_back(tok_rows, norm_scale, gain, grad_normed):
    weighted = gain * grad_normed
    inner = jnp.mean(weighted * tok_rows, axis=-1, keepdims=True)
    grad_rows = norm_scale * weighted - tok_rows * (norm_scale * norm_scale * norm_scale) * inner
    grad_gain = jnp.sum(grad_normed * tok_rows * norm_scale, axis=0)
    return (grad_rows, grad_gain)


def visible(seg_query, pos_query, seg_keys, pos_keys):
    own = (seg_keys[None, :] == seg_query[:, None]) & (pos_keys[None, :] <= pos_query[:, None])
    branch = (
        (seg_keys[None, :] == 0)
        & (seg_query[:, None] > 0)
        & (pos_keys[None, :] < seg_query[:, None] * CLEN)
    )
    return own | branch


def general(
    tokens,
    w_query,
    key_weight,
    value_weight,
    w_out,
    w_gate,
    w_up,
    w_down,
    gain_attn,
    gain_ffn,
    segments,
    positions,
    cotangent,
):
    groups, tok_local, model_width = tokens.shape
    token_count = groups * tok_local
    heads_here = w_query.shape[1] // HEAD_SIZE
    kv_here = key_weight.shape[1] // HEAD_SIZE
    per_kv = heads_here // kv_here
    kv_width = kv_here * HEAD_SIZE
    score_scale = 1.0 / math.sqrt(HEAD_SIZE)
    context_index = lax.axis_index("context")
    first_row = context_index * tok_local
    seg_here = lax.dynamic_slice_in_dim(segments, first_row, tok_local, 1)
    pos_here = lax.dynamic_slice_in_dim(positions, first_row, tok_local, 1)
    w_query, key_weight, value_weight, w_gate, w_up, gain_attn, gain_ffn = (
        lax.all_gather(w_query, "shard", axis=0, tiled=True),
        lax.all_gather(key_weight, "shard", axis=0, tiled=True),
        lax.all_gather(value_weight, "shard", axis=0, tiled=True),
        lax.all_gather(w_gate, "shard", axis=0, tiled=True),
        lax.all_gather(w_up, "shard", axis=0, tiled=True),
        lax.all_gather(gain_attn, "shard", axis=0, tiled=True),
        lax.all_gather(gain_ffn, "shard", axis=0, tiled=True),
    )
    w_out, w_down = (
        lax.all_gather(w_out, "shard", axis=1, tiled=True),
        lax.all_gather(w_down, "shard", axis=1, tiled=True),
    )
    gain_one = gain_attn.astype(jnp.float32)
    gain_two = gain_ffn.astype(jnp.float32)
    tok_rows = tokens.reshape(token_count, model_width).astype(jnp.float32)
    scale_one = lax.rsqrt(jnp.mean(tok_rows * tok_rows, axis=-1, keepdims=True) + norm_eps)
    normed_input = (tok_rows * scale_one * gain_one).astype(jnp.bfloat16)
    cosine_table, sine_values = tables(pos_here.reshape(token_count))
    query_heads_rows = rotary_apply(
        jnp.dot(normed_input, w_query, preferred_element_type=jnp.float32).reshape(
            token_count, heads_here, HEAD_SIZE
        ),
        cosine_table,
        sine_values,
    )
    query_heads_rows = query_heads_rows.astype(jnp.bfloat16).reshape(
        groups, tok_local, heads_here * HEAD_SIZE
    )
    key_rows = rotary_apply(
        jnp.dot(normed_input, key_weight, preferred_element_type=jnp.float32).reshape(
            token_count, kv_here, HEAD_SIZE
        ),
        cosine_table,
        sine_values,
    )
    key_rows = key_rows.astype(jnp.bfloat16).reshape(token_count, kv_width)
    value_rows = jnp.dot(normed_input, value_weight, preferred_element_type=jnp.float32).astype(
        jnp.bfloat16
    )
    keyval = jnp.concatenate([key_rows, value_rows], axis=-1).reshape(
        groups, tok_local, 2 * kv_width
    )
    gathered = lax.all_gather(keyval, "context", axis=1, tiled=True)

    def scores_of(group_queries, group_keyval, seg_query, pos_query, seg_keys, pos_keys):
        grouped_heads = group_queries.reshape(tok_local, kv_here, per_kv, HEAD_SIZE)
        key_head_rows = group_keyval[:, :kv_width].reshape(-1, kv_here, HEAD_SIZE)
        scores = (
            jnp.einsum(
                "bhgd,khd->hgbk", grouped_heads, key_head_rows, preferred_element_type=jnp.float32
            )
            * score_scale
        )
        allowed = visible(seg_query, pos_query, seg_keys, pos_keys)
        return (jnp.where(allowed[None, None], scores, -1e30), grouped_heads, key_head_rows)

    def attend_group(inputs):
        group_queries, group_keyval, seg_query, pos_query, seg_keys, pos_keys = inputs
        scores, grouped_heads, key_head_rows = scores_of(
            group_queries, group_keyval, seg_query, pos_query, seg_keys, pos_keys
        )
        top_score = jnp.max(scores, axis=-1, keepdims=True)
        exponent = jnp.exp(scores - top_score)
        totals = jnp.sum(exponent, axis=-1, keepdims=True)
        soft_weights = (exponent / totals).astype(jnp.bfloat16)
        value_head_rows = group_keyval[:, kv_width:].reshape(-1, kv_here, HEAD_SIZE)
        attended_output = jnp.einsum(
            "hgbk,khd->bhgd", soft_weights, value_head_rows, preferred_element_type=jnp.float32
        )
        return (
            attended_output.reshape(tok_local, heads_here * HEAD_SIZE),
            (top_score + jnp.log(totals))[..., 0],
        )

    attended_output, log_total = lax.map(
        attend_group, (query_heads_rows, gathered, seg_here, pos_here, segments, positions)
    )
    attended_low = attended_output.reshape(token_count, heads_here * HEAD_SIZE).astype(jnp.bfloat16)
    attn_sum = lax.psum(jnp.dot(attended_low, w_out, preferred_element_type=jnp.float32), "tensor")
    middle = tok_rows + attn_sum
    scale_two = lax.rsqrt(jnp.mean(middle * middle, axis=-1, keepdims=True) + norm_eps)
    normed_two = (middle * scale_two * gain_two).astype(jnp.bfloat16)
    gate_proj = jnp.dot(normed_two, w_gate, preferred_element_type=jnp.float32)
    up_proj = jnp.dot(normed_two, w_up, preferred_element_type=jnp.float32)
    sigmoid_gate = jax.nn.sigmoid(gate_proj)
    silu_gate = gate_proj * sigmoid_gate
    hidden = (silu_gate * up_proj).astype(jnp.bfloat16)
    ffn_sum = lax.psum(
        jnp.dot(hidden, w_down, preferred_element_type=jnp.float32).astype(jnp.bfloat16), "tensor"
    ).astype(jnp.float32)
    output = (middle + ffn_sum).astype(jnp.bfloat16).reshape(groups, tok_local, model_width)
    grad_low = cotangent.reshape(token_count, model_width)
    grad_out = grad_low.astype(jnp.float32)
    grad_hidden = contract_cols(grad_low, w_down)
    grad_w_down_t = contract_rows(grad_low, hidden)
    grad_gate = (
        grad_hidden * up_proj * sigmoid_gate * (1.0 + gate_proj * (1.0 - sigmoid_gate))
    ).astype(jnp.bfloat16)
    grad_up = (grad_hidden * silu_gate).astype(jnp.bfloat16)
    grad_w_gate = contract_rows(normed_two, grad_gate)
    grad_w_up = contract_rows(normed_two, grad_up)
    grad_normed_two = lax.psum(
        contract_cols(grad_gate, w_gate) + contract_cols(grad_up, w_up), "tensor"
    )
    back_two, grad_gain_two = norm_back(middle, scale_two, gain_two, grad_normed_two)
    grad_middle = grad_out + back_two
    grad_mid_low = grad_middle.astype(jnp.bfloat16)
    grad_w_out_t = contract_rows(grad_mid_low, attended_low)
    grad_attended = (
        contract_cols(grad_mid_low, w_out)
        .astype(jnp.bfloat16)
        .reshape(groups, tok_local, heads_here * HEAD_SIZE)
    )

    def attend_back(inputs):
        (
            group_queries,
            group_keyval,
            group_grad,
            group_total,
            seg_query,
            pos_query,
            seg_keys,
            pos_keys,
        ) = inputs
        scores, grouped_heads, key_head_rows = scores_of(
            group_queries, group_keyval, seg_query, pos_query, seg_keys, pos_keys
        )
        soft_weights = jnp.exp(scores - group_total[..., None])
        value_head_rows = group_keyval[:, kv_width:].reshape(-1, kv_here, HEAD_SIZE)
        grad_grouped = group_grad.reshape(tok_local, kv_here, per_kv, HEAD_SIZE)
        grad_weights = jnp.einsum(
            "bhgd,khd->hgbk", grad_grouped, value_head_rows, preferred_element_type=jnp.float32
        )
        inner = jnp.sum(soft_weights * grad_weights, axis=-1, keepdims=True)
        grad_scores = (soft_weights * (grad_weights - inner)).astype(jnp.bfloat16)
        grad_queries = (
            jnp.einsum(
                "hgbk,khd->bhgd", grad_scores, key_head_rows, preferred_element_type=jnp.float32
            )
            * score_scale
        )
        grad_keys = (
            jnp.einsum(
                "hgbk,bhgd->khd", grad_scores, grouped_heads, preferred_element_type=jnp.float32
            )
            * score_scale
        )
        grad_values = jnp.einsum(
            "hgbk,bhgd->khd",
            soft_weights.astype(jnp.bfloat16),
            grad_grouped,
            preferred_element_type=jnp.float32,
        )
        grad_keyval = jnp.concatenate(
            [grad_keys.reshape(-1, kv_width), grad_values.reshape(-1, kv_width)], axis=-1
        )
        return (grad_queries.reshape(tok_local, heads_here * HEAD_SIZE), grad_keyval)

    grad_queries, grad_keyval = lax.map(
        attend_back,
        (
            query_heads_rows,
            gathered,
            grad_attended,
            log_total,
            seg_here,
            pos_here,
            segments,
            positions,
        ),
    )
    grad_keyval = lax.psum_scatter(grad_keyval, "context", scatter_dimension=1, tiled=True)
    grad_query_rows = rotate_back(
        grad_queries.reshape(token_count, heads_here, HEAD_SIZE), cosine_table, sine_values
    )
    grad_query_rows = grad_query_rows.astype(jnp.bfloat16).reshape(
        token_count, heads_here * HEAD_SIZE
    )
    grad_key_rows = rotate_back(
        grad_keyval[..., :kv_width].reshape(token_count, kv_here, HEAD_SIZE),
        cosine_table,
        sine_values,
    )
    grad_key_rows = grad_key_rows.astype(jnp.bfloat16).reshape(token_count, kv_width)
    grad_value_rows = (
        grad_keyval[..., kv_width:].reshape(token_count, kv_width).astype(jnp.bfloat16)
    )
    grad_w_query = contract_rows(normed_input, grad_query_rows)
    grad_w_key = contract_rows(normed_input, grad_key_rows)
    grad_w_value = contract_rows(normed_input, grad_value_rows)
    partial_one = (
        contract_cols(grad_query_rows, w_query)
        + contract_cols(grad_key_rows, key_weight)
        + contract_cols(grad_value_rows, value_weight)
    )
    grad_normed = lax.psum(partial_one, "tensor")
    back_one, grad_gain_one = norm_back(tok_rows, scale_one, gain_one, grad_normed)
    tokens_grad = (
        (grad_middle + back_one).astype(jnp.bfloat16).reshape(groups, tok_local, model_width)
    )
    summed = (
        lax.psum_scatter(grad_w_query, ("shard", "context"), scatter_dimension=0, tiled=True),
        lax.psum_scatter(grad_w_key, ("shard", "context"), scatter_dimension=0, tiled=True),
        lax.psum_scatter(grad_w_value, ("shard", "context"), scatter_dimension=0, tiled=True),
        lax.psum_scatter(grad_w_out_t, ("shard", "context"), scatter_dimension=0, tiled=True),
        lax.psum_scatter(grad_w_gate, ("shard", "context"), scatter_dimension=0, tiled=True),
        lax.psum_scatter(grad_w_up, ("shard", "context"), scatter_dimension=0, tiled=True),
        lax.psum_scatter(grad_w_down_t, ("shard", "context"), scatter_dimension=0, tiled=True),
        lax.psum_scatter(grad_gain_one, ("shard", "context"), scatter_dimension=0, tiled=True),
        lax.psum_scatter(grad_gain_two, ("shard", "context"), scatter_dimension=0, tiled=True),
    )
    summed = (
        lax.all_gather(summed[0].astype(jnp.bfloat16), "context", axis=0, tiled=True).astype(
            jnp.float32
        ),
        lax.all_gather(summed[1].astype(jnp.bfloat16), "context", axis=0, tiled=True).astype(
            jnp.float32
        ),
        lax.all_gather(summed[2].astype(jnp.bfloat16), "context", axis=0, tiled=True).astype(
            jnp.float32
        ),
        lax.all_gather(summed[3].astype(jnp.bfloat16), "context", axis=0, tiled=True).astype(
            jnp.float32
        ),
        lax.all_gather(summed[4].astype(jnp.bfloat16), "context", axis=0, tiled=True).astype(
            jnp.float32
        ),
        lax.all_gather(summed[5].astype(jnp.bfloat16), "context", axis=0, tiled=True).astype(
            jnp.float32
        ),
        lax.all_gather(summed[6].astype(jnp.bfloat16), "context", axis=0, tiled=True).astype(
            jnp.float32
        ),
        lax.all_gather(summed[7].astype(jnp.bfloat16), "context", axis=0, tiled=True).astype(
            jnp.float32
        ),
        lax.all_gather(summed[8].astype(jnp.bfloat16), "context", axis=0, tiled=True).astype(
            jnp.float32
        ),
    )
    return (
        output,
        tokens_grad,
        summed[0],
        summed[1],
        summed[2],
        summed[3].T,
        summed[4],
        summed[5],
        summed[6].T,
        summed[7],
        summed[8],
    )


MESH = pl.DeviceIdType.MESH
RUN = 256
PAD = 128
NEG = -1e30
LOG2E = 1.4426950408889634
BF = jnp.bfloat16
F32 = jnp.float32
VLIM = 64 * 1024 * 1024


def mm(a, b):
    return lax.dot_general(a, b, (((1,), (0,)), ((), ())), preferred_element_type=F32)


def mm_nt(a, b):
    return lax.dot_general(a, b, (((1,), (1,)), ((), ())), preferred_element_type=F32)


def mm_tn(a, b):
    return lax.dot_general(a, b, (((0,), (0,)), ((), ())), preferred_element_type=F32)


def iota(shape, axis):
    return lax.broadcasted_iota(jnp.int32, shape, axis)


def one_hot(hit):
    return jnp.where(hit, 1.0, 0.0).astype(BF)


def pad_matrix(heads, flip=False):
    shape = (heads * HEAD_SIZE, heads * PAD)
    if flip:
        row, col = iota(shape[::-1], 1), iota(shape[::-1], 0)
    else:
        row, col = iota(shape, 0), iota(shape, 1)
    lane = col & 127
    part = jnp.where(lane < 64, lane, lane - 16)
    return one_hot((row == (col >> 7) * HEAD_SIZE + part) & ((lane & 63) < 48))


def split_matrix():
    row, col = iota((RUN, RUN), 0), iota((RUN, RUN), 1)
    return one_hot(col == jnp.where(row < 128, 2 * row, 2 * row - 255))


def merge_matrix():
    row, col = iota((RUN, RUN), 0), iota((RUN, RUN), 1)
    return one_hot(col == (row >> 1) + (row & 1) * 128)


def rope_tables(run, cb_ref, sb_ref, cj_ref, sj_ref):
    cb, sb = cb_ref[pl.ds(run, 1), :], sb_ref[pl.ds(run, 1), :]
    cj, sj = cj_ref[...], sj_ref[...]
    return cb * cj - sb * sj, sb * cj + cb * sj


def rope(u, c, s):
    return u * c + pltpu.roll(u, 64, 1) * s


def rope_back(u, c, s):
    return u * c - pltpu.roll(u, 64, 1) * s


def vmem(*shape_dtype):
    return pl.BlockSpec(memory_space=pltpu.VMEM)


def entry_barrier(targets):
    bar = pltpu.get_barrier_semaphore()
    for t in targets:
        pl.semaphore_signal(bar, inc=1, device_id=t, device_id_type=MESH)
    pl.semaphore_wait(bar, len(targets))


def remote(src, dst, send, recv, target):
    return pltpu.make_async_remote_copy(
        src_ref=src, dst_ref=dst, send_sem=send, recv_sem=recv, device_id=target, device_id_type=MESH
    )


def first_kernel(nc, x_ref, dy_h, g_ref, cb_ref, sb_ref, cj_ref, sj_ref, wq_h, wk_h, wv_h, wo_h, wg_h, wu_h, wd_h,
                 xp_ref, dyp_ref, n1_ref, q_ref, kvp_ref, kvc_ref, wp_ref, gf_ref, wo_f, wg_f, wu_f, wd_f,
                 dy_v, wq_s, wk_s, wv_s, g_s, wo_v, wg_v, wu_v, wd_v, kv_send,
                 lsem, ssem, rsem, osem, csem, crem):
    s = lax.axis_index("shard")
    c = lax.axis_index("context")
    dh = g_s.shape[1] // 2
    own = pl.ds(pl.multiple_of(s * dh, dh), dh)
    other = {"shard": 1 - s}
    loads = [
        pltpu.make_async_copy(wq_h, wq_s.at[own], lsem.at[0]),
        pltpu.make_async_copy(wk_h, wk_s.at[:, own], lsem.at[1]),
        pltpu.make_async_copy(wv_h, wv_s.at[:, own], lsem.at[2]),
        pltpu.make_async_copy(g_ref, g_s.at[:, own], lsem.at[3]),
        pltpu.make_async_copy(wo_h, wo_v, lsem.at[4]),
        pltpu.make_async_copy(wg_h, wg_v, lsem.at[5]),
        pltpu.make_async_copy(wu_h, wu_v, lsem.at[6]),
        pltpu.make_async_copy(wd_h, wd_v, lsem.at[7]),
        pltpu.make_async_copy(dy_h, dy_v, lsem.at[8]),
    ]
    for cp in loads:
        cp.start()
    entry_barrier([other] + [{"context": lax.rem(c + i, nc)} for i in range(1, nc)])
    sends = [
        remote(wq_s.at[own], wq_s.at[own], ssem.at[0], rsem.at[0], other),
        remote(wk_s.at[:, own], wk_s.at[:, own], ssem.at[1], rsem.at[1], other),
        remote(wv_s.at[:, own], wv_s.at[:, own], ssem.at[2], rsem.at[2], other),
        remote(g_s.at[:, own], g_s.at[:, own], ssem.at[3], rsem.at[3], other),
        remote(wo_v, wo_f.at[:, own], ssem.at[4], rsem.at[4], other),
        remote(wg_v, wg_f.at[own], ssem.at[5], rsem.at[5], other),
        remote(wu_v, wu_f.at[own], ssem.at[6], rsem.at[6], other),
        remote(wd_v, wd_f.at[:, own], ssem.at[7], rsem.at[7], other),
    ]
    keeps = [
        pltpu.make_async_copy(wo_v, wo_f.at[:, own], osem.at[0]),
        pltpu.make_async_copy(wg_v, wg_f.at[own], osem.at[1]),
        pltpu.make_async_copy(wu_v, wu_f.at[own], osem.at[2]),
        pltpu.make_async_copy(wd_v, wd_f.at[:, own], osem.at[3]),
    ]
    for i in (3, 0, 1, 2, 4, 5, 6, 7):
        loads[i].wait()
        sends[i].start()
        if i >= 4:
            keeps[i - 4].start()
    half = x_ref.shape[0] // 2
    split = split_matrix()
    for i in range(x_ref.shape[0] // RUN):
        xb = mm(split, x_ref[pl.ds(i * RUN, RUN), :])
        xp_ref[pl.ds(i * 128, 128), :] = xb[:128].astype(BF)
        xp_ref[pl.ds(half + i * 128, 128), :] = xb[128:].astype(BF)
        if i == 0:
            sends[3].wait_recv()
        r = lax.rsqrt(jnp.mean(xb * xb, axis=-1, keepdims=True) + norm_eps)
        nb = (xb * r * g_s[0:1, :]).astype(BF)
        n1_ref[pl.ds(i * 128, 128), :] = nb[:128]
        n1_ref[pl.ds(half + i * 128, 128), :] = nb[128:]
    gf_ref[...] = g_s[...]
    hq, hk = wq_s.shape[1] // HEAD_SIZE, wk_s.shape[0] // HEAD_SIZE
    selq, selk = pad_matrix(hq, True), pad_matrix(hk, True)
    nq, nk = hq * PAD, hk * PAD
    for i in range(3):
        sends[i].wait_recv()
    wp_ref[0:nq, :] = mm_nt(selq, wq_s[...]).astype(BF)
    wp_ref[nq : nq + nk, :] = mm(selk, wk_s[...]).astype(BF)
    wp_ref[nq + nk :, :] = mm(selk, wv_s[...]).astype(BF)
    selkv = pad_matrix(2 * hk)
    runs = x_ref.shape[0] // RUN
    per = runs // 2
    kv_copies = []
    for run in range(runs):
        rows = pl.ds(run * RUN, RUN)
        y = mm_nt(n1_ref[rows, :], wp_ref[...])
        ct, st = rope_tables(run, cb_ref, sb_ref, cj_ref, sj_ref)
        for h in range(hq):
            q_ref[rows, h * PAD : (h + 1) * PAD] = rope(y[:, h * PAD : (h + 1) * PAD], ct, st).astype(BF)
        kv = [rope(y[:, nq + h * PAD : nq + (h + 1) * PAD], ct, st).astype(BF) for h in range(hk)]
        kv = jnp.concatenate(kv + [y[:, nq + nk :].astype(BF)], axis=1)
        if run < per:
            kv_send[pl.ds(run * RUN, RUN), :] = mm_nt(kv, selkv).astype(BF)
            mine = pl.ds(pl.multiple_of((c * per + run) * RUN, RUN), RUN)
            for i in range(1, nc):
                cp = remote(kv_send.at[pl.ds(run * RUN, RUN)], kvp_ref.at[mine], csem.at[run, i], crem.at[run, i],
                            {"context": lax.rem(c + i, nc)})
                cp.start()
                kv_copies.append(cp)
            cp = pltpu.make_async_copy(kv_send.at[pl.ds(run * RUN, RUN)], kvp_ref.at[mine], csem.at[run, 0])
            cp.start()
            kv_copies.append(cp)
        else:
            kvc_ref[pl.ds((run - per) * RUN, RUN), :] = kv
    loads[8].wait()
    for i in range(x_ref.shape[0] // RUN):
        b = mm(split, dy_v[pl.ds(i * RUN, RUN), :]).astype(BF)
        dyp_ref[pl.ds(i * 128, 128), :] = b[:128]
        dyp_ref[pl.ds(half + i * 128, 128), :] = b[128:]
    for cp in kv_copies:
        cp.wait()
    for i in range(4):
        keeps[i].wait()
        sends[4 + i].wait_recv()
    for cp in sends:
        cp.wait_send()


class Line:
    F_AT = (8, 9, 10, 12)
    D_AT = (11, 13, 14, 15)

    def __init__(self, n, chunk, pbuf, rbuf, obuf, sems):
        self.n, self.chunk, self.per = n, chunk, RUN // 2 // chunk
        self.count = 16 * self.per
        self.pbuf, self.rbuf, self.obuf = pbuf, rbuf, obuf
        self.rs, self.rr, self.bs, self.br = sems
        self.hop = 3
        self.turn = 2 * (n - 1) * self.hop
        self.slots = self.count + self.turn

    def pieces(self, h, i):
        n, chunk = self.n, self.chunk
        z = lax.axis_index("tensor")
        job = i // self.per
        late = jnp.where((job == 11) | (job > 12), 1, 0)
        row = jnp.where(job < 8, lax.rem(job, 4), jnp.where(late == 1, jnp.maximum(job - 12, 0), jnp.minimum(job - 8, 3)))
        part = jnp.where(job < 8, job // 4, 2 - late)
        off = row * RUN + h * (RUN // 2) + lax.rem(i, self.per) * chunk
        rows = pl.ds(pl.multiple_of(off, chunk), chunk)
        orows = pl.ds(pl.multiple_of(part * (4 * RUN) + off, chunk), chunk)
        place = z if h == 0 else n - 1 - z
        up, down = jnp.minimum(z + 1, n - 1), jnp.maximum(z - 1, 0)
        ahead = {"tensor": up if h == 0 else down}
        back = {"tensor": down if h == 0 else up}
        fwd = remote(self.pbuf.at[rows], self.rbuf.at[rows], self.rs.at[h, i], self.rr.at[h, i], ahead)
        ret = remote(self.obuf.at[orows], self.obuf.at[orows], self.bs.at[h, i], self.br.at[h, i], back)
        return rows, orows, place, fwd, ret

    def reduce_step(self, h, i):
        rows, orows, place, fwd, ret = self.pieces(h, i)
        n = self.n

        @pl.when(place == 0)
        def _():
            fwd.start()

        @pl.when(place > 0)
        def _():
            fwd.wait_recv()
            total = (self.rbuf[rows, :].astype(F32) + self.pbuf[rows, :].astype(F32)).astype(BF)

            @pl.when(place < n - 1)
            def _():
                self.pbuf[rows, :] = total
                fwd.start()

            @pl.when(place == n - 1)
            def _():
                self.obuf[orows, :] = total
                ret.start()

    def spread_step(self, h, i):
        rows, orows, place, fwd, ret = self.pieces(h, i)

        @pl.when(place < self.n - 1)
        def _():
            ret.wait_recv()

        @pl.when((place < self.n - 1) & (place > 0))
        def _():
            ret.start()

    def serve(self, t):
        n = self.n
        z = lax.axis_index("tensor")
        for h in range(2):
            place = z if h == 0 else n - 1 - z
            i = t - place * self.hop

            @pl.when((i >= 0) & (i < self.count))
            def _():
                self.reduce_step(h, i)

            j = t - (2 * (n - 1) - place) * self.hop

            @pl.when((j >= 0) & (j < self.count))
            def _():
                self.spread_step(h, j)

    def sent(self, job, fwd=True, ret=False):
        def step(i, _):
            for h in range(2):
                rows, orows, place, f, r = self.pieces(h, job * self.per + i)
                if fwd:

                    @pl.when(place < self.n - 1)
                    def _():
                        f.wait_send()

                if ret:

                    @pl.when(place > 0)
                    def _():
                        r.wait_send()

            return 0

        lax.fori_loop(0, self.per, step, 0)


def run_items(items, serve):
    total = max(e for spans, _ in items for _, e in spans)

    def step(k, _):
        for spans, body in items:
            hit = functools.reduce(jnp.logical_or, [(k >= lo) & (k < hi) for lo, hi in spans])
            pl.when(hit)(functools.partial(body, k))
        serve(k)
        return 0

    lax.fori_loop(0, total, step, 0)


class Square:
    def __init__(self, rows, cols, src, mine, theirs, spare, out, credit, shard_send, shard_recv, send, recv, store):
        self.src, self.mine, self.theirs, self.res, self.out = src, mine, theirs, theirs, out
        self.r1, self.r2 = [spare[0:2], spare[2:4]], spare[4:6]
        self.credit, self.shard_sems, self.shard_recv, self.send, self.recv, self.store_sem = credit, shard_send, shard_recv, send, recv, store
        self.rows, self.qr, self.cols = rows, rows // 4, cols
        c = lax.axis_index("context")
        self.cy, self.cx = c // 2, lax.rem(c, 2)

    def at(self, y, x, half):
        w = self.cols // 2
        return (pl.ds(pl.multiple_of((2 * y + x) * self.qr, self.qr), self.qr), pl.ds(half * w, w))

    def peer(self, half, first):
        if (half == 0) == first:
            return {"context": 2 * self.cy + 1 - self.cx}
        return {"context": 2 * (1 - self.cy) + self.cx}

    def shard_copy(self):
        return remote(self.src, self.theirs, self.shard_sems, self.shard_recv, {"shard": 1 - lax.axis_index("shard")})

    def outer(self, half):
        if half == 0:
            return [(y, 1 - self.cx) for y in range(2)], [(y, self.cx) for y in range(2)]
        return [(1 - self.cy, x) for x in range(2)], [(self.cy, x) for x in range(2)]

    def p1(self, half, j):
        return remote(self.mine.at[self.at(*self.outer(half)[0][j], half)], self.r1[half][j],
                      self.send.at[0, half, j], self.recv.at[0, half, j], self.peer(half, True))

    def p2(self, half):
        q = (1 - self.cy, self.cx) if half == 0 else (self.cy, 1 - self.cx)
        return remote(self.mine.at[self.at(*q, half)], self.r2[half],
                      self.send.at[1, half, 0], self.recv.at[1, half, 0], self.peer(half, False))

    def p3(self, half):
        at = self.at(self.cy, self.cx, half)
        return remote(self.res.at[at], self.res.at[at], self.send.at[1, half, 1], self.recv.at[1, half, 1], self.peer(half, False))

    def p4(self, half, j):
        at = self.at(*self.outer(half)[1][j], half)
        return remote(self.res.at[at], self.res.at[at], self.send.at[2, half, j], self.recv.at[2, half, j], self.peer(half, True))

    def free(self):
        for t in ({"shard": 1 - lax.axis_index("shard")}, self.peer(0, True), self.peer(0, False)):
            pl.semaphore_signal(self.credit, inc=1, device_id=t, device_id_type=MESH)

    def e0(self):
        pl.semaphore_wait(self.credit, 3)
        self.shard_copy().start()

    def e1(self):
        self.shard_copy().wait_recv()
        step = self.qr

        def add(i, _):
            rows = pl.ds(pl.multiple_of(i * step, step), step)
            self.mine[rows, :] = (self.mine[rows, :].astype(F32) + self.theirs[rows, :].astype(F32)).astype(BF)
            return 0

        lax.fori_loop(0, self.rows // step, add, 0)
        for j in range(2):
            for half in range(2):
                self.p1(half, j).start()

    def e2(self):
        for half in range(2):
            for j in range(2):
                self.p1(half, j).wait_recv()
                at = self.at(*self.outer(half)[1][j], half)
                self.mine[at] = (self.mine[at].astype(F32) + self.r1[half][j][...].astype(F32)).astype(BF)
            self.p2(half).start()

    def e3(self):
        for half in range(2):
            self.p2(half).wait_recv()
            at = self.at(self.cy, self.cx, half)
            self.res[at] = (self.mine[at].astype(F32) + self.r2[half][...].astype(F32)).astype(BF)
            self.p3(half).start()

    def e4(self):
        for half in range(2):
            self.p3(half).wait_recv()
            for j in range(2):
                self.p4(half, j).start()

    def e5(self):
        for half in range(2):
            for j in range(2):
                self.p4(half, j).wait_recv()

    def store(self):
        return pltpu.make_async_copy(self.res, self.out, self.store_sem)

    def done(self):
        self.shard_copy().wait_send()
        for half in range(2):
            for j in range(2):
                self.p1(half, j).wait_send()
                self.p4(half, j).wait_send()
            self.p2(half).wait_send()
            self.p3(half).wait_send()


def line_barrier(n, peers=()):
    z = lax.axis_index("tensor")
    bar = pltpu.get_barrier_semaphore()
    for t in peers:
        pl.semaphore_signal(bar, inc=1, device_id=t, device_id_type=MESH)

    @pl.when(z > 0)
    def _():
        pl.semaphore_signal(bar, inc=1, device_id={"tensor": jnp.maximum(z - 1, 0)}, device_id_type=MESH)

    @pl.when(z < n - 1)
    def _():
        pl.semaphore_signal(bar, inc=1, device_id={"tensor": jnp.minimum(z + 1, n - 1)}, device_id_type=MESH)

    pl.semaphore_wait(bar, len(peers) + jnp.minimum(z, 1) + jnp.minimum(n - 1 - z, 1))


def main_kernel(n, nc, chunk, kbase, qlim, cb_ref, sb_ref, cj_ref, sj_ref, gf_ref, q_ref, kvc_ref, wo_ref,
                kvp_h, xp_h, dyp_h, wg_h, wu_h, wd_h, n1_h, wp_h,
                out_h, tg_h, gg_h, gu_h, gd_h, go_h, gw_h, dm_h, gds_h, fp_h, gains_ref,
                k_s, v_s, s_s, o_v, op_v, lse_v, xs, ys, pbuf, rbuf, obuf, wd, n2, wg, wu, hid, dg, du, gt,
                dk_s, dv_s, do_v, dq_s, delta_s, dqp, dkv_s, go_v, st_o, st_t, st_p, gpart, grecv,
                lsem, ksem, osem, fsem, msem, nsem, qsend, qrecv, gs, gr, rs, rr, bs, br, credits, shard_send, shard_recv, send, recv, store):
    s = lax.axis_index("shard")
    c = lax.axis_index("context")
    rows_here, d = xs.shape
    runs = rows_here // RUN
    per = runs // 2
    half = rows_here // 2
    hk = k_s.shape[0]
    hq = q_ref.shape[1] // PAD
    rep = hq // hk
    blocks = k_s.shape[1] // RUN
    ff = wg.shape[1]
    dh = d // 2
    nq, nk = hq * PAD, hk * PAD
    score = 1.0 / math.sqrt(HEAD_SIZE)
    scale = LOG2E * score
    own = pl.ds(pl.multiple_of(s * dh, dh), dh)
    yours = pl.ds(pl.multiple_of((1 - s) * dh, dh), dh)
    wide = 2 * hk * HEAD_SIZE

    def at(i, size=RUN):
        return pl.ds(pl.multiple_of(i * size, size), size)

    kv_in = [dg.at[pl.ds((b % 4) * RUN, RUN), pl.ds(b // 4 * wide, wide)] for b in range(blocks)]
    key_loads = [pltpu.make_async_copy(kvp_h.at[pl.ds(b * RUN, RUN)], kv_in[b], ksem.at[b]) for b in range(blocks)]
    for cp in key_loads:
        cp.start()
    pairs = [(xp_h, xs), (wg_h, wg), (wu_h, wu), (dyp_h, ys), (wd_h, wd)]
    loads = [pltpu.make_async_copy(a, b, lsem.at[i]) for i, (a, b) in enumerate(pairs)]
    for cp in loads:
        cp.start()
    peers = [{"shard": lax.rem(s + i // nc, 2), "context": lax.rem(c + lax.rem(i, nc), nc)} for i in range(1, 2 * nc)]
    line_barrier(n, peers)
    line = Line(n, chunk, pbuf, rbuf, obuf, (rs, rr, bs, br))
    a_of = lambda job: at(job)
    b_of = lambda job: at(runs + job)
    lane = iota((RUN, PAD), 1)
    for b in range(blocks):
        key_loads[b].wait()
        kv = mm(kv_in[b][...], pad_matrix(2 * hk))
        rows = pl.ds(b * RUN, RUN)
        for g in range(hk):
            k_s[g, rows, :] = kv[:, g * PAD : (g + 1) * PAD].astype(BF)
            v_s[g, rows, :] = jnp.where(lane == 48, 1.0, kv[:, (hk + g) * PAD : (hk + g + 1) * PAD]).astype(BF)
    dk_s[...] = jnp.zeros_like(dk_s)
    dv_s[...] = jnp.zeros_like(dv_s)
    gpart[...] = jnp.zeros_like(gpart)

    def across(total, width, body):
        def step(i, _):
            body(at(i, width))
            return 0

        lax.fori_loop(0, total // width, step, 0)

    def down_rows(start, count, size, body):
        def step(i, _):
            body(pl.ds(pl.multiple_of(start + i * size, size), size), pl.ds(pl.multiple_of(i * size, size), size))
            return 0

        lax.fori_loop(0, count // size, step, 0)

    def head(k, mixed):
        job, h = k // hq, lax.rem(k, hq)
        run = job + per if mixed else job - per
        diff = iota((RUN, RUN), 1) - iota((RUN, RUN), 0)
        rows, cols = at(run), at(h, PAD)
        g = h // rep
        q = q_ref[rows, cols]
        lim = qlim[run]
        top = None
        for b in range(blocks):
            t = mm_nt(q, k_s[g, pl.ds(b * RUN, RUN), :]) * scale
            room = lim - kbase[b]
            if mixed:
                t = t + jnp.where(room >= 0, 0.0, NEG)
            else:
                t = jnp.where(diff <= room, t, NEG)
            s_s[:, b * RUN : (b + 1) * RUN] = t
            top = t if top is None else jnp.maximum(top, t)
        if mixed:
            crow = at(run - per)
            kc = kvc_ref[crow, at(g, PAD)]
            vc = kvc_ref[crow, at(hk + g, PAD)]
            vc = jnp.where(lane == 48, 1.0, vc.astype(F32)).astype(BF)
            t = jnp.where(diff <= 0, mm_nt(q, kc) * scale, NEG)
            s_s[:, blocks * RUN :] = t
            top = jnp.maximum(top, t)
        m = jnp.max(top, axis=1, keepdims=True)
        acc = None
        for b in range(blocks):
            p = jnp.exp2(s_s[:, b * RUN : (b + 1) * RUN] - m).astype(BF)
            o = mm(p, v_s[g, pl.ds(b * RUN, RUN), :])
            acc = o if acc is None else acc + o
        if mixed:
            p = jnp.exp2(s_s[:, blocks * RUN :] - m).astype(BF)
            acc = acc + mm(p, vc)
        total = acc[:, 48:49]
        op_v[rows, cols] = (acc / total).astype(BF)
        lse = jnp.broadcast_to(m + jnp.log2(total), (RUN, PAD)).T
        lse_v[at(run * hq + h, 8), :] = lse[0:8, :]

        @pl.when(h == hq - 1)
        def _():
            o = mm_nt(op_v[rows, :], pad_matrix(hq)).astype(BF)
            o_v[rows, :] = o


            def out(cols):
                pbuf[at(job), cols] = mm(o, wo_ref[:, cols]).astype(BF)

            across(d, 512, out)

    first = runs * hq

    def ffn(k):
        job = (k - first) // 4
        part = lax.rem(k - first, 4)
        run = lax.rem(job + per, runs)
        rows = at(run)

        @pl.when(k == first)
        def _():
            for cp in loads:
                cp.wait()

        @pl.when(part == 0)
        def _():
            def norm(to, sub):
                srows = pl.ds(pl.multiple_of(job * RUN + sub.start, 32), 32)
                mid = xs[to, :].astype(F32) + obuf[srows, :].astype(F32)
                r = lax.rsqrt(jnp.mean(mid * mid, axis=-1, keepdims=True) + norm_eps)
                n2[to, :] = (mid * r * gf_ref[8:9, :]).astype(BF)

            down_rows(run * RUN, RUN, 32, norm)

            def gate(cols):
                s_s[:, cols] = mm(n2[rows, :], wg[:, cols])

            across(ff, 512, gate)

        @pl.when(part == 1)
        def _():
            def up(i, _):
                s_s[:, pl.ds(pl.multiple_of(ff + i * 512, 512), 512)] = mm(n2[rows, :], wu[:, at(i, 512)])
                return 0

            lax.fori_loop(0, ff // 512, up, 0)

        @pl.when(part == 2)
        def _():
            def gated(i, _):
                cols = at(i)
                dhid = mm_nt(ys[rows, :], wd[cols, :])
                gate, up = s_s[:, cols], s_s[:, pl.ds(pl.multiple_of(ff + i * RUN, RUN), RUN)]
                sig = jax.nn.sigmoid(gate)
                silu = gate * sig
                hid[rows, cols] = (silu * up).astype(BF)
                dg[rows, cols] = (dhid * up * sig * (1.0 + gate * (1.0 - sig))).astype(BF)
                du[rows, cols] = (dhid * silu).astype(BF)
                return 0

            lax.fori_loop(0, ff // RUN, gated, 0)

        @pl.when(part == 3)
        def _():
            line.sent(job)

            def normed_two(cols):
                pbuf[at(job), cols] = (mm_nt(dg[rows, :], wg[cols, :]) + mm_nt(du[rows, :], wu[cols, :])).astype(BF)

            across(d, 512, normed_two)
            cp = pltpu.make_async_copy(st_o, fp_h.at[at(job)], osem.at[0])

            @pl.when(job > 0)
            def _():
                cp.wait()

            def project(cols):
                st_o[:, cols] = mm(hid[rows, :], wd[:, cols]).astype(BF)

            across(d, 512, project)
            cp.start()

    second = first + 4 * runs

    def stage(st, sem, dst, value, busy=True):
        cp = pltpu.make_async_copy(st, dst, sem)
        if busy is True:
            cp.wait()
        else:
            pl.when(busy)(cp.wait)

        def fill(cols):
            st[:, cols] = value(cols)

        across(d, 512, fill)
        cp.start()

    def grads_down(k):
        i = k - second
        for j in range(2):
            cols = at(2 * i + j)
            ht = hid[:, cols].T
            stage(st_o, osem.at[0], gds_h.at[cols], lambda to: mm(ht, ys[:, to]).astype(BF))

    def grads_up(k):
        i = k - second - 2
        for j in range(2):
            cols = at(2 * i + j)
            nt = n2[:, cols].T


            def both(to):
                wg[cols, to] = mm(nt, dg[:, to]).astype(BF)
                wu[cols, to] = mm(nt, du[:, to]).astype(BF)

            across(ff, 512, both)

    back = second + 5

    def middle(k):
        job = (k - back) // 5
        run = lax.rem(job + per, runs)
        rows = at(run)
        cp = pltpu.make_async_copy(s_s.at[:, pl.ds(0, d)], dm_h.at[rows], osem.at[1])

        @pl.when(job > 0)
        def _():
            cp.wait()

        def one(to, sub):
            def there(base):
                return pl.ds(pl.multiple_of(base + sub.start, 32), 32)

            mid = xs[to, :].astype(F32) + obuf[there(job * RUN), :].astype(F32)
            r = lax.rsqrt(jnp.mean(mid * mid, axis=-1, keepdims=True) + norm_eps)
            dn = obuf[there((runs + job) * RUN), :].astype(F32)
            w = gf_ref[8:9, :] * dn
            inner = jnp.mean(w * mid, axis=-1, keepdims=True)
            dm = ys[to, :].astype(F32) + r * w - mid * (r * r * r) * inner
            s_s[sub, 0:d] = dm
            gpart[8:16, :] += jnp.sum((dn * mid * r).reshape(4, 8, d), axis=0)
            ys[to, :] = dm.astype(BF)

        down_rows(run * RUN, RUN, 32, one)
        cp.start()
        do = mm_nt(ys[rows, :], wo_ref[...]).astype(BF)
        do_v[rows, :] = mm(do, pad_matrix(hq)).astype(BF)

    width = rep * RUN

    def pair(k, mixed):
        job = (k - back) // 5
        idx = lax.rem(k - back, 5) - 1
        g, part = idx // 2, lax.rem(idx, 2)
        run = lax.rem(job + per, runs)
        rows = at(run)
        diff = iota((RUN, width), 0) - (iota((RUN, width), 1) & (RUN - 1))

        def stack(ref):
            return jnp.concatenate([ref[rows, at(g * rep + j, PAD)] for j in range(rep)], axis=0)

        q, do = stack(q_ref), stack(do_v)

        @pl.when(part == 0)
        def _():
            op = stack(op_v)
            delta_s[0:1, :] = jnp.sum((do.astype(F32) * op.astype(F32)).T, axis=0, keepdims=True)
            dq_s[...] = jnp.zeros_like(dq_s)

        delta = delta_s[0:1, :]
        lse = jnp.concatenate(
            [lse_v[pl.ds(pl.multiple_of((run * hq + g * rep + j) * 8, 8), 1), :] for j in range(rep)], axis=1
        )
        lim = qlim[run]

        def tile(kk, vv, hide):
            p = jnp.exp2(hide(mm_nt(kk, q) * scale - lse))
            ds = (p * (mm_nt(vv, do) - delta)).astype(BF)
            return mm(ds, q), mm(p.astype(BF), do), mm_tn(ds, kk)

        dq = dq_s[...]
        for bb in range(blocks // 2):
            b = part * (blocks // 2) + bb
            room = lim - kbase[b]
            if mixed:
                hide = lambda t: t + jnp.where(room >= 0, 0.0, NEG)
            else:
                hide = lambda t: jnp.where(diff <= room, t, NEG)
            dk, dv, dd = tile(k_s[g, at(b), :], v_s[g, at(b), :], hide)
            dk_s[g, at(b), :] += dk
            dv_s[g, at(b), :] += dv
            dq = dq + dd
        dq_s[...] = dq

        @pl.when(part == 1)
        def _():
            total = dq_s[...]
            ct, st = rope_tables(run, cb_ref, sb_ref, cj_ref, sj_ref)
            if mixed:
                crow = at(run - per)
                dk, dv, dd = tile(kvc_ref[crow, at(g, PAD)], kvc_ref[crow, at(hk + g, PAD)], lambda t: jnp.where(diff <= 0, t, NEG))
                total = total + dd
                dkv_s[rows, at(g, PAD)] = rope_back(dk * score, ct, st).astype(BF)
                dkv_s[rows, at(hk + g, PAD)] = dv.astype(BF)
            for j in range(rep):
                dqp[rows, at(g * rep + j, PAD)] = rope_back(total[j * RUN : (j + 1) * RUN] * score, ct, st).astype(BF)

    def spare(ref, r0, c0, rows, cols, across, count):
        return [ref.at[pl.ds(r0 + i // across * rows, rows), pl.ds(c0 + i % across * cols, cols)] for i in range(count)]

    def square(i, rows, cols, src, mine, theirs, views, out):
        return Square(rows, cols, src, mine, theirs, views, out, credits.at[i], shard_send.at[i], shard_recv.at[i], send.at[i], recv.at[i], store.at[i])

    q4, w4 = dh // 4, ff // 2
    sq_g = square(0, dh, ff, wg.at[yours], wg.at[own], dg.at[pl.ds(0, dh)], spare(n2, 0, 0, q4, w4, 2, 6), gg_h)
    left = spare(n2, 0, 2 * w4, q4, w4, 1, 3) + spare(n2, 3 * q4, 0, q4, w4, 3, 3)
    sq_u = square(1, dh, ff, wu.at[yours], wu.at[own], du.at[pl.ds(0, dh)], left, gu_h)
    f4, d4 = ff // 4, dh // 2
    sq_d = square(2, ff, dh, gds_h.at[:, yours], hid.at[:, pl.ds(0, dh)], gt,
                  spare(n2, dh, 0, f4, d4, 4, 4) + spare(dg, dh, 0, f4, d4, 2, 2), gd_h)
    dq_cols = hq * HEAD_SIZE
    sq_o = square(3, dq_cols, dh, go_v.at[1 - s], go_v.at[s], wg.at[pl.ds(0, dq_cols), pl.ds(0, dh)],
                  spare(wg, dq_cols, 0, dq_cols // 4, d4, 2, 6), go_h)
    gw_cols = dq_cols + wide
    sq_w = square(4, dh, gw_cols, wu.at[yours, pl.ds(0, gw_cols)], wu.at[own, pl.ds(0, gw_cols)], hid.at[pl.ds(0, dh), pl.ds(0, gw_cols)],
                  spare(gt, 0, 0, q4, gw_cols // 2, 2, 6), gw_h)
    down_load = pltpu.make_async_copy(gds_h.at[:, own], hid.at[:, pl.ds(0, dh)], lsem.at[5])
    wp_load = pltpu.make_async_copy(wp_h, wd, lsem.at[6])

    def f_load(job):
        return pltpu.make_async_copy(fp_h.at[at(job)], pbuf.at[at(job)], fsem.at[job])

    def f_start(job):
        line.sent(4 + job)
        f_load(job).start()

    def key_piece(b):
        return ys.at[pl.ds(pl.multiple_of(lax.rem(b, 4) * RUN, RUN), RUN), pl.ds(pl.multiple_of(b // 4 * wide, wide), wide)]

    def key_recv(i, run):
        m = (i - 1) * per + run
        return ys.at[pl.ds(m % 4 * RUN, RUN), pl.ds(dh + m // 4 * wide, wide)]

    def key_copy(i, run):
        to = lax.rem(c + i, nc)
        return remote(key_piece(to * per + run), key_recv(i, run), qsend.at[i, run], qrecv.at[i, run], {"context": to})

    def pack():
        ot = o_v[...].T
        for j in range(2):


            def part(cols, j=j):
                go_v[j, :, cols] = mm(ot, ys[:, pl.ds(pl.multiple_of(j * dh + cols.start, RUN), RUN)]).astype(BF)

            across(dh, RUN, part)
        for i in range(1, nc):
            pl.semaphore_signal(credits.at[5], inc=1, device_id={"context": lax.rem(c + i, nc)}, device_id_type=MESH)

        def one(b, _):
            rows = at(b)
            parts = [(dk_s[g, rows, :] * score).astype(BF) for g in range(hk)]
            parts += [dv_s[g, rows, :].astype(BF) for g in range(hk)]
            value = mm_nt(jnp.concatenate(parts, axis=1), pad_matrix(2 * hk)).astype(BF)
            key_piece(b)[...] = value
            return 0

        lax.fori_loop(0, blocks, one, 0)
        pl.semaphore_wait(credits.at[5], nc - 1)
        for i in range(1, nc):
            for run in range(per):
                key_copy(i, run).start()

    def normed(job):
        rows = at(lax.rem(job + per, runs))
        line.sent(8 + job + jnp.where(job == 3, 1, 0))
        line.sent(4 + job, fwd=False, ret=True)

        def part(cols):
            dn = mm(dqp[rows, :], wd[0:nq, cols]) + mm(dkv_s[rows, :], wd[nq:, cols])
            pbuf[at(job), cols] = dn.astype(BF)

        across(d, 512, part)

    def keys():
        for i in range(1, nc):
            for run in range(per):
                key_copy(i, run).wait_recv()
        selkv = pad_matrix(2 * hk)
        for run in range(per):
            rows = pl.ds(run * RUN, RUN)
            total = mm(key_piece(c * per + run)[...], selkv)
            for i in range(1, nc):
                total = total + mm(key_recv(i, run)[...], selkv)
            ct, st = rope_tables(run, cb_ref, sb_ref, cj_ref, sj_ref)
            for g in range(hk):
                dkv_s[rows, g * PAD : (g + 1) * PAD] = rope_back(total[:, g * PAD : (g + 1) * PAD], ct, st).astype(BF)
            dkv_s[rows, hk * PAD :] = total[:, hk * PAD :].astype(BF)

    tile_v = hid.at[:, pl.ds(dh, RUN)]

    def tile_load(i):
        return pltpu.make_async_copy(n1_h.at[:, at(i)], tile_v, nsem)

    def grads_in(k):
        i = k - into

        @pl.when(i == 0)
        def _():
            def pack_rows(to, sub):
                du[to, 0:dq_cols] = mm_nt(dqp[to, :], pad_matrix(hq)).astype(BF)
                du[to, dq_cols:gw_cols] = mm_nt(dkv_s[to, :], pad_matrix(2 * hk)).astype(BF)

            down_rows(0, rows_here, RUN, pack_rows)

        for j in range(2):
            tile_load(2 * i + j).wait()
            nt = tile_v[...].T


            def part(cols, j=j):
                wu[at(2 * i + j), cols] = mm(nt, du[:, cols]).astype(BF)

            across(gw_cols, gw_cols // 2, part)

            @pl.when(2 * i + j + 1 < d // RUN)
            def _():
                tile_load(2 * i + j + 1).start()

    def halves(i, body):
        for j in range(2):

            def step(m, _, j=j):
                natural = pl.ds(pl.multiple_of(j * half + i * 128 + m * 32, 32), 32)
                by_job = lambda part: pl.ds(pl.multiple_of(part * rows_here + (1 - j) * half + i * 128 + m * 32, 32), 32)
                body(natural, by_job, pl.ds(pl.multiple_of(j * 128 + m * 32, 32), 32))
                return 0

            lax.fori_loop(0, 4, step, 0)

    def output(k):
        i = k - outs

        def one(natural, by_job, to):
            total = xs[natural, :].astype(F32) + obuf[by_job(0), :].astype(F32)
            st_p[to, :] = (total + obuf[by_job(2), :].astype(F32)).astype(BF)

        halves(i, one)
        stage(st_o, osem.at[0], out_h.at[at(i)], lambda cols: mm(merge_matrix(), st_p[:, cols]).astype(BF), i > 0)

    def m_load(i, j):
        src = dm_h.at[pl.ds(pl.multiple_of(j * half + i * 128, 128), 128)]
        return pltpu.make_async_copy(src, s_s.at[pl.ds(j * 128, 128), pl.ds(0, d)], msem.at[j])

    def finals(i):
        for j in range(2):
            m_load(i, j).wait()

        def one(natural, by_job, to):
            x = xs[natural, :].astype(F32)
            dn = obuf[by_job(1), :].astype(F32)
            r = lax.rsqrt(jnp.mean(x * x, axis=-1, keepdims=True) + norm_eps)
            w = gf_ref[0:1, :] * dn
            inner = jnp.mean(w * x, axis=-1, keepdims=True)
            st_p[to, :] = (s_s[to, 0:d] + (r * w - x * (r * r * r) * inner)).astype(BF)
            gpart[0:8, :] += jnp.sum((dn * x * r).reshape(4, 8, d), axis=0)

        halves(i, one)

        @pl.when(i + 1 < runs)
        def _():
            for j in range(2):
                m_load(i + 1, j).start()

        cp = pltpu.make_async_copy(st_t, tg_h.at[at(i)], osem.at[2])

        @pl.when(i > 0)
        def _():
            cp.wait()

        def fill(cols):
            st_t[:, cols] = mm(merge_matrix(), st_p[:, cols]).astype(BF)

        across(d, 512, fill)
        cp.start()

    packed = back + 5 * runs
    into = packed + 3
    outs = into + 4
    lag = hq - 1

    def due(job):
        return (line.per * (job + 1) - 1 + line.turn) // 2 + lag + 1

    begins = [back + 5 * job for job in range(runs)]
    items = [([(0, per * hq)], lambda k: head(k, True)), ([(per * hq, first)], lambda k: head(k, False)), ([(first, second)], ffn),
             ([(second, second + 2)], grads_down), ([(second + 2, back)], grads_up), ([(b, b + 1) for b in begins], middle),
             ([(b + 1, b + 5) for b in begins[:per]], lambda k: pair(k, True)),
             ([(b + 1, b + 5) for b in begins[per:]], lambda k: pair(k, False)),
             ([(into, into + 3)], grads_in), ([(outs, outs + runs)], output)]
    fin = due(Line.D_AT[per])

    def begin_down():
        pltpu.make_async_copy(st_o, gds_h.at[pl.ds(0, RUN)], osem.at[0]).wait()
        down_load.start()
        wp_load.start()

    def free_three():
        for sq in (sq_g, sq_u, sq_d):
            sq.free()
        for sq in (sq_g, sq_u, sq_d):
            sq.e0()

    def store_start(sq):
        def body():
            sq.e5()
            sq.store().start()

        return body

    def dm_begin():
        pltpu.make_async_copy(s_s.at[:, pl.ds(0, d)], dm_h.at[pl.ds(0, RUN)], osem.at[1]).wait()
        for j in range(2):
            m_load(0, j).start()

    def first_e1():
        down_load.wait()
        sq_d.e1()

    def give_o():
        sq_g.store().wait()
        sq_g.done()
        sq_o.free()

    def give_w():
        sq_d.store().wait()
        sq_d.done()
        sq_w.free()

    def release_u():
        sq_u.store().wait()
        sq_u.done()

    def number(k, steps):
        return sum(jnp.where(k >= step, 1, 0) for step in steps[1:])

    events = [(second + 2, begin_down), (second + 4, free_three)]
    at_f = [4 * Line.F_AT[job] + lag - 2 for job in range(runs)]
    events += [
        (39, first_e1), (40, sq_g.e1), (41, sq_d.e2), (41, sq_u.e1), (42, sq_g.e2), (43, sq_d.e3), (44, sq_u.e2), (44, sq_g.e3),
        (45, wp_load.wait), (45, sq_d.e4), (46, sq_g.e4), (47, sq_u.e3), (48, store_start(sq_d)), (49, store_start(sq_g)),
        (50, sq_u.e4), (51, give_o), (53, store_start(sq_u)), (54, give_w), (55, release_u),
        (packed, pack), (packed, lambda: tile_load(0).start()), (packed, dm_begin), (packed + 1, sq_o.e0),
        (packed + 2, keys),
        (61, sq_o.e1), (62, sq_w.e0), (63, sq_o.e2), (63, sq_w.e1), (65, sq_w.e2), (65, sq_o.e3), (67, sq_w.e3), (67, sq_o.e4), (69, sq_w.e4),
        (69, store_start(sq_o)), (71, store_start(sq_w)),
    ]
    items += [([(k, k + 1)], functools.partial(lambda e, k: e(), e)) for k, e in events]
    at_normed = (45, 50, packed + 2, packed + 3)
    items.append(([(k, k + 1) for k in at_f], lambda k: f_start(number(k, at_f))))
    items.append(([(k + 1, k + 2) for k in at_f], lambda k: f_load(number(k, at_f)).wait()))
    items.append(([(k, k + 1) for k in at_normed], lambda k: normed(number(k, at_normed))))
    end = line.slots // 2 + lag
    items.append(([(fin, fin + 2), (end, end + 2)], lambda k: finals(jnp.where(k < end, k - fin, k - end + 2))))

    def serve(k):
        def tick(j, _):
            line.serve(2 * (k - lag) + j)
            return 0

        lax.fori_loop(0, 2, tick, 0)

    run_items(items, serve)
    me = s * nc + c
    sums = jnp.concatenate(
        [jnp.broadcast_to(jnp.sum(gpart[k * 8 : (k + 1) * 8, :], axis=0, keepdims=True), (8, d)) for k in range(2)], axis=0
    )
    grecv[me] = sums
    gcopies = []
    for i, t in enumerate(peers):
        cp = remote(grecv.at[me], grecv.at[me], gs.at[i], gr.at[i], t)
        cp.start()
        gcopies.append(cp)

    def rest(job, _):
        line.sent(jnp.where(job < runs, job, job + runs), fwd=False, ret=True)
        return 0

    lax.fori_loop(0, 3 * runs, rest, 0)
    for job in Line.D_AT:
        line.sent(job)
    for sq in (sq_o, sq_w):
        sq.store().wait()
        sq.done()
    for i in range(1, nc):
        for run in range(per):
            key_copy(i, run).wait_send()
    pltpu.make_async_copy(st_o, out_h.at[pl.ds(0, RUN)], osem.at[0]).wait()
    pltpu.make_async_copy(st_t, tg_h.at[pl.ds(0, RUN)], osem.at[2]).wait()
    for cp in gcopies:
        cp.wait()
    total = grecv[0]
    for i in range(1, 2 * nc):
        total = total + grecv[i]
    gpart[...] = total
    gains_ref[...] = gpart[:, own]


def finish_kernel(out_h, tg_h, gw_h, go_h, gg_h, gu_h, gd_h, out_f, tg_f, gq_f, gk_f, gv_f, go_f, gg_f, gu_f, gd_f,
                  out_v, tg_v, gw_v, go_v, gg_v, gu_v, gd_v, q_v, kv_v, o_v, g_v, u_v, d_v, lsem, ssem):
    kw = gk_f.shape[0]
    nq = gw_h.shape[1] - 2 * kw
    pairs = [(gg_h, gg_v), (gu_h, gu_v), (gd_h, gd_v), (gw_h, gw_v), (go_h, go_v), (out_h, out_v), (tg_h, tg_v)]
    loads = [pltpu.make_async_copy(a, b, lsem.at[i]) for i, (a, b) in enumerate(pairs)]
    for cp in loads:
        cp.start()
    stores = [
        pltpu.make_async_copy(a, b, ssem.at[i])
        for i, (a, b) in enumerate([(g_v, gg_f), (u_v, gu_f), (d_v, gd_f), (q_v, gq_f), (kv_v.at[0:kw], gk_f), (kv_v.at[kw:], gv_f),
                                    (o_v, go_f), (out_v, out_f), (tg_v, tg_f)])
    ]

    def widen(src, dst, width):
        def step(i, _):
            rows = pl.ds(pl.multiple_of(i * 32, 32), 32)
            dst[rows, :] = src[rows, 0:width].astype(F32)
            return 0

        lax.fori_loop(0, src.shape[0] // 32, step, 0)

    for i, (src, dst) in enumerate([(gg_v, g_v), (gu_v, u_v), (gd_v, d_v)]):
        loads[i].wait()
        widen(src, dst, src.shape[1])
        stores[i].start()
    loads[5].wait()
    stores[7].start()
    loads[6].wait()
    stores[8].start()
    loads[3].wait()
    widen(gw_v, q_v, nq)
    stores[3].start()
    for i in range(gw_v.shape[0] // PAD):
        kv_v[:, i * PAD : (i + 1) * PAD] = gw_v[i * PAD : (i + 1) * PAD, nq:].astype(F32).T
    stores[4].start()
    stores[5].start()
    loads[4].wait()
    widen(go_v, o_v, go_v.shape[1])
    stores[6].start()
    for cp in stores:
        cp.wait()


def fast(
    tokens, w_query, key_weight, value_weight, w_out, w_gate, w_up, w_down, gain_attn, gain_ffn, segments, positions, cotangent, n, nc
):
    _, rows, d = tokens.shape
    half = rows // 2
    runs = rows // RUN
    per = runs // 2
    prompt = segments.shape[1] // 2
    blocks = prompt // RUN
    dq, dk = w_query.shape[1], key_weight.shape[1]
    hq, hk = dq // HEAD_SIZE, dk // HEAD_SIZE
    nq, nk = hq * PAD, hk * PAD
    ff = w_gate.shape[1]
    dh = d // 2
    c = lax.axis_index("context")
    x = tokens.reshape(rows, d)
    dy = cotangent.reshape(rows, d)
    kbase = positions[0, 0 :: 2 * RUN]
    seg_here = lax.dynamic_slice_in_dim(segments[0], c * rows, rows, 0)
    pos_here = lax.dynamic_slice_in_dim(positions[0], c * rows, rows, 0)
    qbase = jnp.concatenate([pos_here[0 :: 2 * RUN], pos_here[1 :: 2 * RUN]])
    qlim = jnp.concatenate([pos_here[0 :: 2 * RUN], seg_here[1 :: 2 * RUN] * CLEN - 1])
    freq = np.exp(np.arange(HEAD_SIZE // 2, dtype=np.float32) * np.float32(-2.0 * math.log(rope_base) / HEAD_SIZE)).astype(np.float32)
    lanes = np.zeros((PAD,), np.float32)
    lanes[0:48] = freq
    lanes[64:112] = freq
    sign = np.where(np.arange(PAD) < 64, -1.0, 1.0).astype(np.float32)
    inner = np.arange(RUN, dtype=np.float64)[:, None] * lanes[None, :].astype(np.float64)
    cj = jnp.asarray(np.cos(inner).astype(np.float32))
    sj = jnp.asarray((np.sin(inner) * sign).astype(np.float32))
    angle = qbase.astype(F32)[:, None] * jnp.asarray(lanes)[None, :]
    cb = jnp.cos(angle)
    sb = jnp.sin(angle) * jnp.asarray(sign)[None, :]
    gains = jnp.concatenate([jnp.broadcast_to(g.astype(F32)[None, :], (8, dh)) for g in (gain_attn, gain_ffn)], axis=0)

    V = pl.BlockSpec(memory_space=pltpu.VMEM)
    S = pl.BlockSpec(memory_space=pltpu.SMEM)
    A = pl.BlockSpec(memory_space=pl.ANY)
    sds = jax.ShapeDtypeStruct
    DMA = pltpu.SemaphoreType.DMA

    def call(kernel, ins, outs, scratch, collective=None, flops=0):
        params = dict(vmem_limit_bytes=VLIM - 64 * 1024)
        if collective is not None:
            params.update(collective_id=collective, has_side_effects=True)
        args = [a for a, _ in ins]
        return pl.pallas_call(
            kernel,
            out_shape=[o for o, _ in outs],
            in_specs=[sp for _, sp in ins],
            out_specs=[sp for _, sp in outs],
            scratch_shapes=scratch,
            compiler_params=pltpu.CompilerParams(**params),
            cost_estimate=pl.CostEstimate(flops=flops, bytes_accessed=0, transcendentals=0),
        )(*args)

    rope_in = [(cb, V), (sb, V), (cj, V), (sj, V)]
    xp, dyp, n1, q, kvp, kvc, wp, gf, wo, wg, wu, wd = call(
        functools.partial(first_kernel, nc),
        [(x, V), (dy, A), (gains, A)] + rope_in + [(w_query, A), (key_weight.T, A), (value_weight.T, A), (w_out, A), (w_gate, A), (w_up, A), (w_down, A)],
        [
            (sds((rows, d), BF), V), (sds((rows, d), BF), V), (sds((rows, d), BF), V), (sds((rows, nq), BF), V),
            (sds((prompt, 2 * dk), BF), A), (sds((half, 2 * nk), BF), V), (sds((nq + 2 * nk, d), BF), V), (sds((16, d), F32), V),
            (sds((dq, d), BF), A), (sds((d, ff), BF), A), (sds((d, ff), BF), A), (sds((ff, d), BF), A),
        ],
        [
            pltpu.VMEM((rows, d), BF), pltpu.VMEM((d, dq), BF), pltpu.VMEM((dk, d), BF), pltpu.VMEM((dk, d), BF), pltpu.VMEM((16, d), F32),
            pltpu.VMEM((dq, dh), BF), pltpu.VMEM((dh, ff), BF), pltpu.VMEM((dh, ff), BF), pltpu.VMEM((ff, dh), BF),
            pltpu.VMEM((half, 2 * dk), BF),
            DMA((9,)), DMA((8,)), DMA((8,)), DMA((4,)), DMA((per, nc)), DMA((per, nc)),
        ],
        collective=0, flops=60 * 10**9,
    )

    chunk = 16
    count = 16 * (RUN // 2 // chunk)
    U = pltpu.VMEM((rows, d), BF)
    W = pltpu.VMEM((d, ff), BF)
    H = pltpu.VMEM((rows, ff), BF)
    KV = pltpu.VMEM((hk, prompt, PAD), BF)
    KVF = pltpu.VMEM((hk, prompt, PAD), F32)
    width = hq // hk * RUN
    out, tg, gg, gu, gd, go, gw, _, _, _, gains_grad = call(
        functools.partial(main_kernel, n, nc, chunk),
        [(kbase, S), (qlim, S)] + rope_in
        + [(gf, V), (q, V), (kvc, V), (wo, V), (kvp, A), (xp, A), (dyp, A), (wg, A), (wu, A), (wd, A), (n1, A), (wp, A)],
        [(sds((rows, d), BF), A), (sds((rows, d), BF), A), (sds((dh, ff), BF), A), (sds((dh, ff), BF), A), (sds((ff, dh), BF), A),
         (sds((dq, dh), BF), A), (sds((dh, dq + 2 * dk), BF), A), (sds((rows, d), F32), A), (sds((ff, d), BF), A), (sds((rows, d), BF), A),
         (sds((16, dh), F32), V)],
        [KV, KV, pltpu.VMEM((RUN, prompt + RUN), F32), pltpu.VMEM((rows, dq), BF), pltpu.VMEM((rows, nq), BF), pltpu.VMEM((runs * hq * 8, RUN), F32),
         U, U, U, U, pltpu.VMEM((3 * rows, d), BF), pltpu.VMEM((ff, d), BF), U, W, W, H, H, H, pltpu.VMEM((ff, dh), BF),
         KVF, KVF, pltpu.VMEM((rows, nq), BF), pltpu.VMEM((width, PAD), F32), pltpu.VMEM((8, width), F32), pltpu.VMEM((rows, nq), BF),
         pltpu.VMEM((rows, 2 * nk), BF), pltpu.VMEM((2, dq, dh), BF), pltpu.VMEM((RUN, d), BF), pltpu.VMEM((RUN, d), BF), pltpu.VMEM((RUN, d), BF),
         pltpu.VMEM((16, d), F32), pltpu.VMEM((2 * nc, 16, d), F32),
         DMA((7,)), DMA((blocks,)), DMA((3,)), DMA((runs,)), DMA((2,)), DMA, DMA((nc, per)), DMA((nc, per)), DMA((2 * nc - 1,)), DMA((2 * nc - 1,))]
        + [DMA((2, count))] * 4
        + [pltpu.SemaphoreType.REGULAR((6,)), DMA((5,)), DMA((5,)), DMA((5, 3, 2, 2)), DMA((5, 3, 2, 2)), DMA((5,))],
        collective=1, flops=300 * 10**9,
    )
    shapes = [(rows, d), (rows, d), (dh, dq + 2 * dk), (dq, dh), (dh, ff), (dh, ff), (ff, dh)]
    wide = [(dh, dq), (2 * dk, dh), (dq, dh), (dh, ff), (dh, ff), (ff, dh)]
    finals = [(dh, dq), (dk, dh), (dk, dh), (dq, dh), (dh, ff), (dh, ff), (ff, dh)]
    out, tg, gq, gk, gv, go, gg, gu, gd = call(
        finish_kernel,
        [(a, A) for a in (out, tg, gw, go, gg, gu, gd)],
        [(sds((rows, d), BF), A), (sds((rows, d), BF), A)] + [(sds(shape, F32), A) for shape in finals],
        [pltpu.VMEM(shape, BF) for shape in shapes] + [pltpu.VMEM(shape, F32) for shape in wide] + [DMA((7,)), DMA((9,))],
    )
    return out[None], tg[None], gq, gk.T, gv.T, go, gg, gu, gd, gains_grad[0], gains_grad[8]


def body(mesh, *args):
    tokens, w_query, segments = args[0], args[1], args[10]
    n, nc = mesh.shape["tensor"], mesh.shape["context"]
    rows = tokens.shape[1]
    if (tokens.shape[0] == 1 and rows % (4 * CLEN) == 0 and n == 4 and nc == 4 and mesh.shape["shard"] == 2
            and segments.shape[1] == rows * nc):
        return fast(*args, n, nc)
    return general(*args)


def solution(mesh):
    in_specs = (
        P("shard", "context", None),
        P("shard", "tensor"),
        P("shard", "tensor"),
        P("shard", "tensor"),
        P("tensor", "shard"),
        P("shard", "tensor"),
        P("shard", "tensor"),
        P("tensor", "shard"),
        P("shard"),
        P("shard"),
        P("shard", None),
        P("shard", None),
        P("shard", "context", None),
    )
    out_specs = (
        P("shard", "context", None),
        P("shard", "context", None),
        P("shard", "tensor"),
        P("shard", "tensor"),
        P("shard", "tensor"),
        P("tensor", "shard"),
        P("shard", "tensor"),
        P("shard", "tensor"),
        P("tensor", "shard"),
        P("shard"),
        P("shard"),
    )
    return jax.shard_map(functools.partial(body, mesh), mesh=mesh, in_specs=in_specs, out_specs=out_specs, check_vma=False)
```

profile of v0, /device:TPU:1, one launch (start us, length us, event | category | flops | bytes accessed | tf_op | source)
XLA Modules:
  0.0 423.0 jit_solution(2529075215895322135)
XLA Ops:
  0.6 1.3 slice.19
  2.0 0.7 constant_dynamic-slice_fusion
  2.7 0.1 slice.21
  2.8 0.1 slice.22
  2.9 0.1 slice.20
  2.9 0.6 add_convert_fusion
  3.5 1.4 fusion
  4.9 0.7 broadcast_in_dim.8
  5.6 0.7 broadcast_in_dim.9
  6.3 0.6 pad_maximum_fusion.g_ref
  6.9 35.0 %shard_map.248 = (bf16[1024,1536]{1,0:T(8,128)(2,1)}, bf16[1024,1536]{1,0:T(8,128)(2,1)}, bf16[1024,1536]{1,0:T(8,128)(2,1)}, bf16[1024,512]{1,0:T(8,128)(2,1)},...) custom-call(bf16[1024,1536]{1,0:T(8,128)(2,1)} %bitcast.14, ...), custom_call_target="tpu_custom_call" | custom-call | flops 60000002048 | tf_op jit(solution)/shard_map/pallas_call | solution.py:1496
  41.9 367.5 %shard_map.249 = (bf16[1024,1536]{1,0:T(8,128)(2,1)}, bf16[1024,1536]{1,0:T(8,128)(2,1)}, bf16[768,1024]{1,0:T(8,128)(2,1)}, bf16[768,1024]{1,0:T(8,128)(2,1)}, ...) custom-call(s32[8]{0:T(128)} %bitcast.22, ...), custom_call_target="tpu_custom_call" | custom-call | flops 299999985664 | tf_op jit(solution)/shard_map/pallas_call | solution.py:1496
  409.4 1.4 slice_reduce_fusion
  410.8 12.0 %shard_map.250 = (bf16[1024,1536]{1,0:T(8,128)(2,1)}, bf16[1024,1536]{1,0:T(8,128)(2,1)}, f32[768,384]{1,0:T(8,128)}, f32[192,768]{1,0:T(8,128)}, f32[192,768]{1...) custom-call(bf16[1024,1536]{1,0:T(8,128)(2,1)} %get-tuple-element.52.out_h, ...), custom_call_target="tpu_custom_call" | custom-call | tf_op jit(solution)/shard_map/pallas_call | solution.py:1496
  (1 shorter events, 0.0 us)
where the time goes:
time: 424 us; the launch traced here: 423 us
  Pallas kernels  415 us (98%)
  local copies, waits for them, and re-layouts  5.03 us (1%)
    pallas_call x3, Pallas kernels, call(): pl.pallas_call(kernel, out_shape=[o for o, _ in outs], in_specs=[sp for _...  415 us

commit v1 on v0

--- a/solution.py
+++ b/solution.py
@@ -560,6 +560,7 @@
         self.count = 16 * self.per
         self.pbuf, self.rbuf, self.obuf = pbuf, rbuf, obuf
         self.rs, self.rr, self.bs, self.br = sems
+        self.ticks = 32 // chunk
         self.hop = 3
         self.turn = 2 * (n - 1) * self.hop
         self.slots = self.count + self.turn
@@ -1287,7 +1288,7 @@
     lag = hq - 1
 
     def due(job):
-        return (line.per * (job + 1) - 1 + line.turn) // 2 + lag + 1
+        return (line.per * (job + 1) - 1 + line.turn) // line.ticks + lag + 1
 
     begins = [back + 5 * job for job in range(runs)]
     items = [([(0, per * hq)], lambda k: head(k, True)), ([(per * hq, first)], lambda k: head(k, False)), ([(first, second)], ffn),
@@ -1305,7 +1306,7 @@
     def free_three():
         for sq in (sq_g, sq_u, sq_d):
             sq.free()
-        for sq in (sq_g, sq_u, sq_d):
+        for sq in (sq_d, sq_g, sq_u):
             sq.e0()
 
     def store_start(sq):
@@ -1344,28 +1345,27 @@
     events = [(second + 2, begin_down), (second + 4, free_three)]
     at_f = [4 * Line.F_AT[job] + lag - 2 for job in range(runs)]
     events += [
-        (39, first_e1), (40, sq_g.e1), (41, sq_d.e2), (41, sq_u.e1), (42, sq_g.e2), (43, sq_d.e3), (44, sq_u.e2), (44, sq_g.e3),
-        (45, wp_load.wait), (45, sq_d.e4), (46, sq_g.e4), (47, sq_u.e3), (48, store_start(sq_d)), (49, store_start(sq_g)),
-        (50, sq_u.e4), (51, give_o), (53, store_start(sq_u)), (54, give_w), (55, release_u),
-        (packed, pack), (packed, lambda: tile_load(0).start()), (packed, dm_begin), (packed + 1, sq_o.e0),
-        (packed + 2, keys),
-        (61, sq_o.e1), (62, sq_w.e0), (63, sq_o.e2), (63, sq_w.e1), (65, sq_w.e2), (65, sq_o.e3), (67, sq_w.e3), (67, sq_o.e4), (69, sq_w.e4),
-        (69, store_start(sq_o)), (71, store_start(sq_w)),
+        (38, first_e1), (40, sq_g.e1), (41, sq_d.e2), (42, sq_u.e1), (43, sq_g.e2), (44, sq_d.e3), (45, wp_load.wait), (46, sq_u.e2), (47, sq_g.e3),
+        (48, sq_d.e4), (49, sq_u.e3), (50, sq_g.e4), (52, store_start(sq_d)), (53, sq_u.e4), (54, give_w), (55, store_start(sq_g)),
+        (57, store_start(sq_u)), (57, give_o), (59, release_u),
+        (packed, pack), (packed, lambda: tile_load(0).start()), (packed, dm_begin), (packed + 2, keys), (packed + 2, sq_o.e0),
+        (61, sq_o.e1), (62, sq_w.e0), (63, sq_o.e2), (64, sq_w.e1), (65, sq_o.e3), (66, sq_w.e2), (67, sq_o.e4), (68, sq_w.e3),
+        (69, store_start(sq_o)), (70, sq_w.e4), (73, store_start(sq_w)),
     ]
     items += [([(k, k + 1)], functools.partial(lambda e, k: e(), e)) for k, e in events]
     at_normed = (45, 50, packed + 2, packed + 3)
     items.append(([(k, k + 1) for k in at_f], lambda k: f_start(number(k, at_f))))
     items.append(([(k + 1, k + 2) for k in at_f], lambda k: f_load(number(k, at_f)).wait()))
     items.append(([(k, k + 1) for k in at_normed], lambda k: normed(number(k, at_normed))))
-    end = line.slots // 2 + lag
+    end = -(-line.slots // line.ticks) + lag
     items.append(([(fin, fin + 2), (end, end + 2)], lambda k: finals(jnp.where(k < end, k - fin, k - end + 2))))
 
     def serve(k):
         def tick(j, _):
-            line.serve(2 * (k - lag) + j)
+            line.serve(line.ticks * (k - lag) + j)
             return 0
 
-        lax.fori_loop(0, 2, tick, 0)
+        lax.fori_loop(0, line.ticks, tick, 0)
 
     run_items(items, serve)
     me = s * nc + c

time: 424 us -> 401 us (0.946)
  Pallas kernels: 415 us -> 392 us
    pallas_call x3, Pallas kernels: 415 us -> 392 us  [call(): pl.pallas_call(kernel, out_shape=[o for o, _ in outs], in_specs=[sp for _...]
where the time goes in v1:
time: 401 us
  Pallas kernels  392 us (98%)
  local copies, waits for them, and re-layouts  5.03 us (1%)
    pallas_call x3, Pallas kernels, call(): pl.pallas_call(kernel, out_shape=[o for o, _ in outs], in_specs=[sp for _...  392 us

profile of v1, /device:TPU:1, one launch (start us, length us, event | category | flops | bytes accessed | tf_op | source)
XLA Modules:
  0.0 400.8 jit_solution(8744880980672941083)
XLA Ops:
  0.6 1.3 slice.19
  2.0 0.7 constant_dynamic-slice_fusion
  2.7 0.1 slice.21
  2.8 0.1 slice.22
  2.9 0.1 slice.20
  2.9 0.6 add_convert_fusion
  3.5 1.4 fusion
  4.9 0.7 broadcast_in_dim.8
  5.6 0.7 broadcast_in_dim.9
  6.3 0.6 pad_maximum_fusion.g_ref
  6.9 35.0 %shard_map.248 = (bf16[1024,1536]{1,0:T(8,128)(2,1)}, bf16[1024,1536]{1,0:T(8,128)(2,1)}, bf16[1024,1536]{1,0:T(8,128)(2,1)}, bf16[1024,512]{1,0:T(8,128)(2,1)},...) custom-call(bf16[1024,1536]{1,0:T(8,128)(2,1)} %bitcast.14, ...), custom_call_target="tpu_custom_call" | custom-call | flops 60000002048 | tf_op jit(solution)/shard_map/pallas_call | solution.py:1496
  41.9 345.2 %shard_map.249 = (bf16[1024,1536]{1,0:T(8,128)(2,1)}, bf16[1024,1536]{1,0:T(8,128)(2,1)}, bf16[768,1024]{1,0:T(8,128)(2,1)}, bf16[768,1024]{1,0:T(8,128)(2,1)}, ...) custom-call(s32[8]{0:T(128)} %bitcast.22, ...), custom_call_target="tpu_custom_call" | custom-call | flops 299999985664 | tf_op jit(solution)/shard_map/pallas_call | solution.py:1496
  387.2 1.4 slice_reduce_fusion
  388.5 12.0 %shard_map.250 = (bf16[1024,1536]{1,0:T(8,128)(2,1)}, bf16[1024,1536]{1,0:T(8,128)(2,1)}, f32[768,384]{1,0:T(8,128)}, f32[192,768]{1,0:T(8,128)}, f32[192,768]{1...) custom-call(bf16[1024,1536]{1,0:T(8,128)(2,1)} %get-tuple-element.52.out_h, ...), custom_call_target="tpu_custom_call" | custom-call | tf_op jit(solution)/shard_map/pallas_call | solution.py:1496
  (1 shorter events, 0.0 us)

commit v2 on v1

--- a/solution.py
+++ b/solution.py
@@ -460,15 +460,17 @@
         pltpu.make_async_copy(wq_h, wq_s.at[own], lsem.at[0]),
         pltpu.make_async_copy(wk_h, wk_s.at[:, own], lsem.at[1]),
         pltpu.make_async_copy(wv_h, wv_s.at[:, own], lsem.at[2]),
-        pltpu.make_async_copy(g_ref, g_s.at[:, own], lsem.at[3]),
+        None,
         pltpu.make_async_copy(wo_h, wo_v, lsem.at[4]),
         pltpu.make_async_copy(wg_h, wg_v, lsem.at[5]),
         pltpu.make_async_copy(wu_h, wu_v, lsem.at[6]),
         pltpu.make_async_copy(wd_h, wd_v, lsem.at[7]),
         pltpu.make_async_copy(dy_h, dy_v, lsem.at[8]),
     ]
-    for cp in loads:
+    for cp in loads[:3] + loads[4:]:
         cp.start()
+    for i in range(2):
+        g_s[8 * i : 8 * i + 8, own] = jnp.broadcast_to(g_ref[i : i + 1, :], (8, dh))
     entry_barrier([other] + [{"context": lax.rem(c + i, nc)} for i in range(1, nc)])
     sends = [
         remote(wq_s.at[own], wq_s.at[own], ssem.at[0], rsem.at[0], other),
@@ -487,7 +489,8 @@
         pltpu.make_async_copy(wd_v, wd_f.at[:, own], osem.at[3]),
     ]
     for i in (3, 0, 1, 2, 4, 5, 6, 7):
-        loads[i].wait()
+        if i != 3:
+            loads[i].wait()
         sends[i].start()
         if i >= 4:
             keeps[i - 4].start()
@@ -518,12 +521,10 @@
     kv_copies = []
     for run in range(runs):
         rows = pl.ds(run * RUN, RUN)
-        y = mm_nt(n1_ref[rows, :], wp_ref[...])
+        y = mm_nt(n1_ref[rows, :], wp_ref[nq:, :])
         ct, st = rope_tables(run, cb_ref, sb_ref, cj_ref, sj_ref)
-        for h in range(hq):
-            q_ref[rows, h * PAD : (h + 1) * PAD] = rope(y[:, h * PAD : (h + 1) * PAD], ct, st).astype(BF)
-        kv = [rope(y[:, nq + h * PAD : nq + (h + 1) * PAD], ct, st).astype(BF) for h in range(hk)]
-        kv = jnp.concatenate(kv + [y[:, nq + nk :].astype(BF)], axis=1)
+        kv = [rope(y[:, h * PAD : (h + 1) * PAD], ct, st).astype(BF) for h in range(hk)]
+        kv = jnp.concatenate(kv + [y[:, nk:].astype(BF)], axis=1)
         if run < per:
             kv_send[pl.ds(run * RUN, RUN), :] = mm_nt(kv, selkv).astype(BF)
             mine = pl.ds(pl.multiple_of((c * per + run) * RUN, RUN), RUN)
@@ -537,6 +538,12 @@
             kv_copies.append(cp)
         else:
             kvc_ref[pl.ds((run - per) * RUN, RUN), :] = kv
+    for run in range(runs):
+        rows = pl.ds(run * RUN, RUN)
+        y = mm_nt(n1_ref[rows, :], wp_ref[0:nq, :])
+        ct, st = rope_tables(run, cb_ref, sb_ref, cj_ref, sj_ref)
+        for h in range(hq):
+            q_ref[rows, h * PAD : (h + 1) * PAD] = rope(y[:, h * PAD : (h + 1) * PAD], ct, st).astype(BF)
     loads[8].wait()
     for i in range(x_ref.shape[0] // RUN):
         b = mm(split, dy_v[pl.ds(i * RUN, RUN), :]).astype(BF)
@@ -1143,15 +1150,15 @@
         to = lax.rem(c + i, nc)
         return remote(key_piece(to * per + run), key_recv(i, run), qsend.at[i, run], qrecv.at[i, run], {"context": to})
 
+    def grad_out(j):
+        ot = o_v[...].T
+
+        def part(cols):
+            go_v[j, :, cols] = mm(ot, ys[:, pl.ds(pl.multiple_of(j * dh + cols.start, RUN), RUN)]).astype(BF)
+
+        across(dh, RUN, part)
+
     def pack():
-        ot = o_v[...].T
-        for j in range(2):
-
-
-            def part(cols, j=j):
-                go_v[j, :, cols] = mm(ot, ys[:, pl.ds(pl.multiple_of(j * dh + cols.start, RUN), RUN)]).astype(BF)
-
-            across(dh, RUN, part)
         for i in range(1, nc):
             pl.semaphore_signal(credits.at[5], inc=1, device_id={"context": lax.rem(c + i, nc)}, device_id_type=MESH)
 
@@ -1165,8 +1172,8 @@
 
         lax.fori_loop(0, blocks, one, 0)
         pl.semaphore_wait(credits.at[5], nc - 1)
-        for i in range(1, nc):
-            for run in range(per):
+        for run in range(per):
+            for i in range(1, nc):
                 key_copy(i, run).start()
 
     def normed(job):
@@ -1180,20 +1187,18 @@
 
         across(d, 512, part)
 
-    def keys():
+    def keys(run):
         for i in range(1, nc):
-            for run in range(per):
-                key_copy(i, run).wait_recv()
+            key_copy(i, run).wait_recv()
         selkv = pad_matrix(2 * hk)
-        for run in range(per):
-            rows = pl.ds(run * RUN, RUN)
-            total = mm(key_piece(c * per + run)[...], selkv)
-            for i in range(1, nc):
-                total = total + mm(key_recv(i, run)[...], selkv)
-            ct, st = rope_tables(run, cb_ref, sb_ref, cj_ref, sj_ref)
-            for g in range(hk):
-                dkv_s[rows, g * PAD : (g + 1) * PAD] = rope_back(total[:, g * PAD : (g + 1) * PAD], ct, st).astype(BF)
-            dkv_s[rows, hk * PAD :] = total[:, hk * PAD :].astype(BF)
+        rows = pl.ds(run * RUN, RUN)
+        total = mm(key_piece(c * per + run)[...], selkv)
+        for i in range(1, nc):
+            total = total + mm(key_recv(i, run)[...], selkv)
+        ct, st = rope_tables(run, cb_ref, sb_ref, cj_ref, sj_ref)
+        for g in range(hk):
+            dkv_s[rows, g * PAD : (g + 1) * PAD] = rope_back(total[:, g * PAD : (g + 1) * PAD], ct, st).astype(BF)
+        dkv_s[rows, hk * PAD :] = total[:, hk * PAD :].astype(BF)
 
     tile_v = hid.at[:, pl.ds(dh, RUN)]
 
@@ -1283,7 +1288,7 @@
         cp.start()
 
     packed = back + 5 * runs
-    into = packed + 3
+    into = packed + 4
     outs = into + 4
     lag = hq - 1
 
@@ -1348,12 +1353,12 @@
         (38, first_e1), (40, sq_g.e1), (41, sq_d.e2), (42, sq_u.e1), (43, sq_g.e2), (44, sq_d.e3), (45, wp_load.wait), (46, sq_u.e2), (47, sq_g.e3),
         (48, sq_d.e4), (49, sq_u.e3), (50, sq_g.e4), (52, store_start(sq_d)), (53, sq_u.e4), (54, give_w), (55, store_start(sq_g)),
         (57, store_start(sq_u)), (57, give_o), (59, release_u),
-        (packed, pack), (packed, lambda: tile_load(0).start()), (packed, dm_begin), (packed + 2, keys), (packed + 2, sq_o.e0),
-        (61, sq_o.e1), (62, sq_w.e0), (63, sq_o.e2), (64, sq_w.e1), (65, sq_o.e3), (66, sq_w.e2), (67, sq_o.e4), (68, sq_w.e3),
+        (53, lambda: grad_out(0)), (54, lambda: grad_out(1)), (packed, pack), (packed, lambda: tile_load(0).start()), (packed, dm_begin), (packed + 2, lambda: keys(0)), (packed + 2, sq_o.e0), (packed + 3, lambda: keys(1)),
+        (61, sq_o.e1), (63, sq_o.e2), (64, sq_w.e0), (65, sq_w.e1), (65, sq_o.e3), (67, sq_w.e2), (67, sq_o.e4), (68, sq_w.e3),
         (69, store_start(sq_o)), (70, sq_w.e4), (73, store_start(sq_w)),
     ]
     items += [([(k, k + 1)], functools.partial(lambda e, k: e(), e)) for k, e in events]
-    at_normed = (45, 50, packed + 2, packed + 3)
+    at_normed = (45, 50, packed + 2, packed + 4)
     items.append(([(k, k + 1) for k in at_f], lambda k: f_start(number(k, at_f))))
     items.append(([(k + 1, k + 2) for k in at_f], lambda k: f_load(number(k, at_f)).wait()))
     items.append(([(k, k + 1) for k in at_normed], lambda k: normed(number(k, at_normed))))
@@ -1480,7 +1485,7 @@
     angle = qbase.astype(F32)[:, None] * jnp.asarray(lanes)[None, :]
     cb = jnp.cos(angle)
     sb = jnp.sin(angle) * jnp.asarray(sign)[None, :]
-    gains = jnp.concatenate([jnp.broadcast_to(g.astype(F32)[None, :], (8, dh)) for g in (gain_attn, gain_ffn)], axis=0)
+    gains = jnp.stack([gain_attn, gain_ffn]).astype(F32)
 
     V = pl.BlockSpec(memory_space=pltpu.VMEM)
     S = pl.BlockSpec(memory_space=pltpu.SMEM)
@@ -1506,7 +1511,7 @@
     rope_in = [(cb, V), (sb, V), (cj, V), (sj, V)]
     xp, dyp, n1, q, kvp, kvc, wp, gf, wo, wg, wu, wd = call(
         functools.partial(first_kernel, nc),
-        [(x, V), (dy, A), (gains, A)] + rope_in + [(w_query, A), (key_weight.T, A), (value_weight.T, A), (w_out, A), (w_gate, A), (w_up, A), (w_down, A)],
+        [(x, V), (dy, A), (gains, V)] + rope_in + [(w_query, A), (key_weight.T, A), (value_weight.T, A), (w_out, A), (w_gate, A), (w_up, A), (w_down, A)],
         [
             (sds((rows, d), BF), V), (sds((rows, d), BF), V), (sds((rows, d), BF), V), (sds((rows, nq), BF), V),
             (sds((prompt, 2 * dk), BF), A), (sds((half, 2 * nk), BF), V), (sds((nq + 2 * nk, d), BF), V), (sds((16, d), F32), V),

time: 401 us -> 393 us (0.980)
  Pallas kernels: 392 us -> 384 us
    pallas_call x3, Pallas kernels: 392 us -> 384 us  [call(): pl.pallas_call(kernel, out_shape=[o for o, _ in outs], in_specs=[sp for _...]
where the time goes in v2:
time: 393 us; the launch traced here: 392 us
  Pallas kernels  384 us (98%)
  local copies, waits for them, and re-layouts  5.03 us (1%)
    pallas_call x3, Pallas kernels, call(): pl.pallas_call(kernel, out_shape=[o for o, _ in outs], in_specs=[sp for _...  384 us

profile of v2, /device:TPU:1, one launch (start us, length us, event | category | flops | bytes accessed | tf_op | source)
XLA Modules:
  0.0 392.0 jit_solution(689213534526603081)
XLA Ops:
  0.6 1.3 slice.19
  2.0 0.7 stack.9
  2.7 0.7 stack.10
  3.3 0.6 maximum_convert_fusion.g_ref
  3.9 0.7 constant_dynamic-slice_fusion
  4.6 0.1 slice.21
  4.7 0.1 slice.22
  4.8 0.1 slice.20
  4.9 0.6 add_convert_fusion
  5.5 1.4 fusion
  6.9 34.5 %shard_map.248 = (bf16[1024,1536]{1,0:T(8,128)(2,1)}, bf16[1024,1536]{1,0:T(8,128)(2,1)}, bf16[1024,1536]{1,0:T(8,128)(2,1)}, bf16[1024,512]{1,0:T(8,128)(2,1)},...) custom-call(bf16[1024,1536]{1,0:T(8,128)(2,1)} %bitcast.14, ...), custom_call_target="tpu_custom_call" | custom-call | flops 60000002048 | tf_op jit(solution)/shard_map/pallas_call | solution.py:1501
  41.4 337.0 %shard_map.249 = (bf16[1024,1536]{1,0:T(8,128)(2,1)}, bf16[1024,1536]{1,0:T(8,128)(2,1)}, bf16[768,1024]{1,0:T(8,128)(2,1)}, bf16[768,1024]{1,0:T(8,128)(2,1)}, ...) custom-call(s32[8]{0:T(128)} %bitcast.22, ...), custom_call_target="tpu_custom_call" | custom-call | flops 299999985664 | tf_op jit(solution)/shard_map/pallas_call | solution.py:1501
  378.4 1.4 slice_reduce_fusion
  379.8 12.0 %shard_map.250 = (bf16[1024,1536]{1,0:T(8,128)(2,1)}, bf16[1024,1536]{1,0:T(8,128)(2,1)}, f32[768,384]{1,0:T(8,128)}, f32[192,768]{1,0:T(8,128)}, f32[192,768]{1...) custom-call(bf16[1024,1536]{1,0:T(8,128)(2,1)} %get-tuple-element.52.out_h, ...), custom_call_target="tpu_custom_call" | custom-call | tf_op jit(solution)/shard_map/pallas_call | solution.py:1501
  (1 shorter events, 0.0 us)

commit v3 on v2

--- a/solution.py
+++ b/solution.py
@@ -416,8 +416,14 @@
     return one_hot(col == (row >> 1) + (row & 1) * 128)
 
 
-def rope_tables(run, cb_ref, sb_ref, cj_ref, sj_ref):
-    cb, sb = cb_ref[pl.ds(run, 1), :], sb_ref[pl.ds(run, 1), :]
+def first_of(ref, run, per):
+    start = lax.axis_index("context") * (2 * per * RUN)
+    return ref[0, start + run % per * (2 * RUN) + run // per]
+
+
+def rope_tables(run, per, pos_ref, cb_ref, sb_ref, cj_ref, sj_ref):
+    base = first_of(pos_ref, run, per) // RUN
+    cb, sb = cb_ref[pl.ds(base, 1), :], sb_ref[pl.ds(base, 1), :]
     cj, sj = cj_ref[...], sj_ref[...]
     return cb * cj - sb * sj, sb * cj + cb * sj
 
@@ -447,10 +453,10 @@
     )
 
 
-def first_kernel(nc, x_ref, dy_h, g_ref, cb_ref, sb_ref, cj_ref, sj_ref, wq_h, wk_h, wv_h, wo_h, wg_h, wu_h, wd_h,
-                 xp_ref, dyp_ref, n1_ref, q_ref, kvp_ref, kvc_ref, wp_ref, gf_ref, wo_f, wg_f, wu_f, wd_f,
-                 dy_v, wq_s, wk_s, wv_s, g_s, wo_v, wg_v, wu_v, wd_v, kv_send,
-                 lsem, ssem, rsem, osem, csem, crem):
+def first_kernel(nc, x_ref, dy_h, g_ref, pos_ref, cb_ref, sb_ref, cj_ref, sj_ref, wq_h, wk_h, wv_h, wo_h, wg_h, wu_h, wd_h,
+                 xp_h, dyp_h, n1_h, q_ref, kvp_ref, kvc_ref, wp_h, gf_ref, wo_f, wg_f, wu_f, wd_f,
+                 xp_ref, dyp_ref, n1_ref, wp_ref, dy_v, wq_s, wk_s, wv_s, g_s, wo_v, wg_v, wu_v, wd_v, kv_send,
+                 lsem, ssem, rsem, osem, csem, crem, esem):
     s = lax.axis_index("shard")
     c = lax.axis_index("context")
     dh = g_s.shape[1] // 2
@@ -507,6 +513,9 @@
         n1_ref[pl.ds(i * 128, 128), :] = nb[:128]
         n1_ref[pl.ds(half + i * 128, 128), :] = nb[128:]
     gf_ref[...] = g_s[...]
+    exits = [pltpu.make_async_copy(a, b, esem.at[i]) for i, (a, b) in enumerate([(xp_ref, xp_h), (n1_ref, n1_h), (wp_ref, wp_h), (dyp_ref, dyp_h)])]
+    exits[0].start()
+    exits[1].start()
     hq, hk = wq_s.shape[1] // HEAD_SIZE, wk_s.shape[0] // HEAD_SIZE
     selq, selk = pad_matrix(hq, True), pad_matrix(hk, True)
     nq, nk = hq * PAD, hk * PAD
@@ -515,6 +524,7 @@
     wp_ref[0:nq, :] = mm_nt(selq, wq_s[...]).astype(BF)
     wp_ref[nq : nq + nk, :] = mm(selk, wk_s[...]).astype(BF)
     wp_ref[nq + nk :, :] = mm(selk, wv_s[...]).astype(BF)
+    exits[2].start()
     selkv = pad_matrix(2 * hk)
     runs = x_ref.shape[0] // RUN
     per = runs // 2
@@ -522,7 +532,7 @@
     for run in range(runs):
         rows = pl.ds(run * RUN, RUN)
         y = mm_nt(n1_ref[rows, :], wp_ref[nq:, :])
-        ct, st = rope_tables(run, cb_ref, sb_ref, cj_ref, sj_ref)
+        ct, st = rope_tables(run, per, pos_ref, cb_ref, sb_ref, cj_ref, sj_ref)
         kv = [rope(y[:, h * PAD : (h + 1) * PAD], ct, st).astype(BF) for h in range(hk)]
         kv = jnp.concatenate(kv + [y[:, nk:].astype(BF)], axis=1)
         if run < per:
@@ -541,7 +551,7 @@
     for run in range(runs):
         rows = pl.ds(run * RUN, RUN)
         y = mm_nt(n1_ref[rows, :], wp_ref[0:nq, :])
-        ct, st = rope_tables(run, cb_ref, sb_ref, cj_ref, sj_ref)
+        ct, st = rope_tables(run, per, pos_ref, cb_ref, sb_ref, cj_ref, sj_ref)
         for h in range(hq):
             q_ref[rows, h * PAD : (h + 1) * PAD] = rope(y[:, h * PAD : (h + 1) * PAD], ct, st).astype(BF)
     loads[8].wait()
@@ -549,7 +559,8 @@
         b = mm(split, dy_v[pl.ds(i * RUN, RUN), :]).astype(BF)
         dyp_ref[pl.ds(i * 128, 128), :] = b[:128]
         dyp_ref[pl.ds(half + i * 128, 128), :] = b[128:]
-    for cp in kv_copies:
+    exits[3].start()
+    for cp in kv_copies + exits:
         cp.wait()
     for i in range(4):
         keeps[i].wait()
@@ -796,7 +807,7 @@
     pl.semaphore_wait(bar, len(peers) + jnp.minimum(z, 1) + jnp.minimum(n - 1 - z, 1))
 
 
-def main_kernel(n, nc, chunk, kbase, qlim, cb_ref, sb_ref, cj_ref, sj_ref, gf_ref, q_ref, kvc_ref, wo_ref,
+def main_kernel(n, nc, chunk, seg_ref, pos_ref, cb_ref, sb_ref, cj_ref, sj_ref, gf_ref, q_ref, kvc_ref, wo_ref,
                 kvp_h, xp_h, dyp_h, wg_h, wu_h, wd_h, n1_h, wp_h,
                 out_h, tg_h, gg_h, gu_h, gd_h, go_h, gw_h, dm_h, gds_h, fp_h, gains_ref,
                 k_s, v_s, s_s, o_v, op_v, lse_v, xs, ys, pbuf, rbuf, obuf, wd, n2, wg, wu, hid, dg, du, gt,
@@ -823,6 +834,9 @@
 
     def at(i, size=RUN):
         return pl.ds(pl.multiple_of(i * size, size), size)
+
+    def limit(run):
+        return jnp.where(run < per, first_of(pos_ref, run, per), first_of(seg_ref, run, per) * CLEN - 1)
 
     kv_in = [dg.at[pl.ds((b % 4) * RUN, RUN), pl.ds(b // 4 * wide, wide)] for b in range(blocks)]
     key_loads = [pltpu.make_async_copy(kvp_h.at[pl.ds(b * RUN, RUN)], kv_in[b], ksem.at[b]) for b in range(blocks)]
@@ -870,11 +884,11 @@
         rows, cols = at(run), at(h, PAD)
         g = h // rep
         q = q_ref[rows, cols]
-        lim = qlim[run]
+        lim = limit(run)
         top = None
         for b in range(blocks):
             t = mm_nt(q, k_s[g, pl.ds(b * RUN, RUN), :]) * scale
-            room = lim - kbase[b]
+            room = lim - pos_ref[0, 2 * RUN * b]
             if mixed:
                 t = t + jnp.where(room >= 0, 0.0, NEG)
             else:
@@ -1076,7 +1090,7 @@
         lse = jnp.concatenate(
             [lse_v[pl.ds(pl.multiple_of((run * hq + g * rep + j) * 8, 8), 1), :] for j in range(rep)], axis=1
         )
-        lim = qlim[run]
+        lim = limit(run)
 
         def tile(kk, vv, hide):
             p = jnp.exp2(hide(mm_nt(kk, q) * scale - lse))
@@ -1086,7 +1100,7 @@
         dq = dq_s[...]
         for bb in range(blocks // 2):
             b = part * (blocks // 2) + bb
-            room = lim - kbase[b]
+            room = lim - pos_ref[0, 2 * RUN * b]
             if mixed:
                 hide = lambda t: t + jnp.where(room >= 0, 0.0, NEG)
             else:
@@ -1100,7 +1114,7 @@
         @pl.when(part == 1)
         def _():
             total = dq_s[...]
-            ct, st = rope_tables(run, cb_ref, sb_ref, cj_ref, sj_ref)
+            ct, st = rope_tables(run, per, pos_ref, cb_ref, sb_ref, cj_ref, sj_ref)
             if mixed:
                 crow = at(run - per)
                 dk, dv, dd = tile(kvc_ref[crow, at(g, PAD)], kvc_ref[crow, at(hk + g, PAD)], lambda t: jnp.where(diff <= 0, t, NEG))
@@ -1195,7 +1209,7 @@
         total = mm(key_piece(c * per + run)[...], selkv)
         for i in range(1, nc):
             total = total + mm(key_recv(i, run)[...], selkv)
-        ct, st = rope_tables(run, cb_ref, sb_ref, cj_ref, sj_ref)
+        ct, st = rope_tables(run, per, pos_ref, cb_ref, sb_ref, cj_ref, sj_ref)
         for g in range(hk):
             dkv_s[rows, g * PAD : (g + 1) * PAD] = rope_back(total[:, g * PAD : (g + 1) * PAD], ct, st).astype(BF)
         dkv_s[rows, hk * PAD :] = total[:, hk * PAD :].astype(BF)
@@ -1466,14 +1480,8 @@
     nq, nk = hq * PAD, hk * PAD
     ff = w_gate.shape[1]
     dh = d // 2
-    c = lax.axis_index("context")
     x = tokens.reshape(rows, d)
     dy = cotangent.reshape(rows, d)
-    kbase = positions[0, 0 :: 2 * RUN]
-    seg_here = lax.dynamic_slice_in_dim(segments[0], c * rows, rows, 0)
-    pos_here = lax.dynamic_slice_in_dim(positions[0], c * rows, rows, 0)
-    qbase = jnp.concatenate([pos_here[0 :: 2 * RUN], pos_here[1 :: 2 * RUN]])
-    qlim = jnp.concatenate([pos_here[0 :: 2 * RUN], seg_here[1 :: 2 * RUN] * CLEN - 1])
     freq = np.exp(np.arange(HEAD_SIZE // 2, dtype=np.float32) * np.float32(-2.0 * math.log(rope_base) / HEAD_SIZE)).astype(np.float32)
     lanes = np.zeros((PAD,), np.float32)
     lanes[0:48] = freq
@@ -1482,10 +1490,10 @@
     inner = np.arange(RUN, dtype=np.float64)[:, None] * lanes[None, :].astype(np.float64)
     cj = jnp.asarray(np.cos(inner).astype(np.float32))
     sj = jnp.asarray((np.sin(inner) * sign).astype(np.float32))
-    angle = qbase.astype(F32)[:, None] * jnp.asarray(lanes)[None, :]
-    cb = jnp.cos(angle)
-    sb = jnp.sin(angle) * jnp.asarray(sign)[None, :]
-    gains = jnp.stack([gain_attn, gain_ffn]).astype(F32)
+    starts = np.arange(16, dtype=np.float64)[:, None] * RUN * lanes[None, :].astype(np.float64)
+    cb = jnp.asarray(np.cos(starts).astype(np.float32))
+    sb = jnp.asarray((np.sin(starts) * sign).astype(np.float32))
+    gains = jnp.where(np.arange(2)[:, None] == 0, gain_attn[None, :], gain_ffn[None, :]).astype(F32)
 
     V = pl.BlockSpec(memory_space=pltpu.VMEM)
     S = pl.BlockSpec(memory_space=pltpu.SMEM)
@@ -1508,20 +1516,21 @@
             cost_estimate=pl.CostEstimate(flops=flops, bytes_accessed=0, transcendentals=0),
         )(*args)
 
-    rope_in = [(cb, V), (sb, V), (cj, V), (sj, V)]
+    rope_in = [(positions, S), (cb, V), (sb, V), (cj, V), (sj, V)]
     xp, dyp, n1, q, kvp, kvc, wp, gf, wo, wg, wu, wd = call(
         functools.partial(first_kernel, nc),
         [(x, V), (dy, A), (gains, V)] + rope_in + [(w_query, A), (key_weight.T, A), (value_weight.T, A), (w_out, A), (w_gate, A), (w_up, A), (w_down, A)],
         [
-            (sds((rows, d), BF), V), (sds((rows, d), BF), V), (sds((rows, d), BF), V), (sds((rows, nq), BF), V),
-            (sds((prompt, 2 * dk), BF), A), (sds((half, 2 * nk), BF), V), (sds((nq + 2 * nk, d), BF), V), (sds((16, d), F32), V),
+            (sds((rows, d), BF), A), (sds((rows, d), BF), A), (sds((rows, d), BF), A), (sds((rows, nq), BF), V),
+            (sds((prompt, 2 * dk), BF), A), (sds((half, 2 * nk), BF), V), (sds((nq + 2 * nk, d), BF), A), (sds((16, d), F32), V),
             (sds((dq, d), BF), A), (sds((d, ff), BF), A), (sds((d, ff), BF), A), (sds((ff, d), BF), A),
         ],
         [
+            pltpu.VMEM((rows, d), BF), pltpu.VMEM((rows, d), BF), pltpu.VMEM((rows, d), BF), pltpu.VMEM((nq + 2 * nk, d), BF),
             pltpu.VMEM((rows, d), BF), pltpu.VMEM((d, dq), BF), pltpu.VMEM((dk, d), BF), pltpu.VMEM((dk, d), BF), pltpu.VMEM((16, d), F32),
             pltpu.VMEM((dq, dh), BF), pltpu.VMEM((dh, ff), BF), pltpu.VMEM((dh, ff), BF), pltpu.VMEM((ff, dh), BF),
             pltpu.VMEM((half, 2 * dk), BF),
-            DMA((9,)), DMA((8,)), DMA((8,)), DMA((4,)), DMA((per, nc)), DMA((per, nc)),
+            DMA((9,)), DMA((8,)), DMA((8,)), DMA((4,)), DMA((per, nc)), DMA((per, nc)), DMA((4,)),
         ],
         collective=0, flops=60 * 10**9,
     )
@@ -1536,7 +1545,7 @@
     width = hq // hk * RUN
     out, tg, gg, gu, gd, go, gw, _, _, _, gains_grad = call(
         functools.partial(main_kernel, n, nc, chunk),
-        [(kbase, S), (qlim, S)] + rope_in
+        [(segments, S)] + rope_in
         + [(gf, V), (q, V), (kvc, V), (wo, V), (kvp, A), (xp, A), (dyp, A), (wg, A), (wu, A), (wd, A), (n1, A), (wp, A)],
         [(sds((rows, d), BF), A), (sds((rows, d), BF), A), (sds((dh, ff), BF), A), (sds((dh, ff), BF), A), (sds((ff, dh), BF), A),
          (sds((dq, dh), BF), A), (sds((dh, dq + 2 * dk), BF), A), (sds((rows, d), F32), A), (sds((ff, d), BF), A), (sds((rows, d), BF), A),

time: 393 us -> 384 us (0.977)
  Pallas kernels: 384 us -> 380 us
where the time goes in v3:
time: 384 us; the launch traced here: 383 us
  Pallas kernels  380 us (99%)
    pallas_call x3, Pallas kernels, call(): pl.pallas_call(kernel, out_shape=[o for o, _ in outs], in_specs=[sp for _...  380 us

profile of v3, /device:TPU:1, one launch (start us, length us, event | category | flops | bytes accessed | tf_op | source)
XLA Modules:
  0.0 383.3 jit_solution(6755773157962961864)
XLA Ops:
  0.6 1.4 fusion.g_ref
  2.0 30.7 %shard_map.257 = (bf16[1024,1536]{1,0:T(8,128)(2,1)}, bf16[1024,1536]{1,0:T(8,128)(2,1)}, bf16[1024,1536]{1,0:T(8,128)(2,1)}, bf16[1024,512]{1,0:T(8,128)(2,1)},...) custom-call(bf16[1024,1536]{1,0:T(8,128)(2,1)} %bitcast.8, ...), custom_call_target="tpu_custom_call" | custom-call | flops 60000002048 | tf_op jit(solution)/shard_map/pallas_call | solution.py:1509
  32.7 337.0 %shard_map.258 = (bf16[1024,1536]{1,0:T(8,128)(2,1)}, bf16[1024,1536]{1,0:T(8,128)(2,1)}, bf16[768,1024]{1,0:T(8,128)(2,1)}, bf16[768,1024]{1,0:T(8,128)(2,1)}, ...) custom-call(s32[1,4096]{1,0:T(1,128)} %seg_ref.1, ...), custom_call_target="tpu_custom_call" | custom-call | flops 299999985664 | tf_op jit(solution)/shard_map/pallas_call | solution.py:1509
  369.7 1.4 slice_reduce_fusion
  371.1 12.0 %shard_map.259 = (bf16[1024,1536]{1,0:T(8,128)(2,1)}, bf16[1024,1536]{1,0:T(8,128)(2,1)}, f32[768,384]{1,0:T(8,128)}, f32[192,768]{1,0:T(8,128)}, f32[192,768]{1...) custom-call(bf16[1024,1536]{1,0:T(8,128)(2,1)} %get-tuple-element.52.out_h, ...), custom_call_target="tpu_custom_call" | custom-call | tf_op jit(solution)/shard_map/pallas_call | solution.py:1509

commit v4 on v3

--- a/solution.py
+++ b/solution.py
@@ -494,12 +494,10 @@
         pltpu.make_async_copy(wu_v, wu_f.at[own], osem.at[2]),
         pltpu.make_async_copy(wd_v, wd_f.at[:, own], osem.at[3]),
     ]
-    for i in (3, 0, 1, 2, 4, 5, 6, 7):
+    for i in (3, 0, 1, 2):
         if i != 3:
             loads[i].wait()
         sends[i].start()
-        if i >= 4:
-            keeps[i - 4].start()
     half = x_ref.shape[0] // 2
     split = split_matrix()
     for i in range(x_ref.shape[0] // RUN):
@@ -525,6 +523,10 @@
     wp_ref[nq : nq + nk, :] = mm(selk, wk_s[...]).astype(BF)
     wp_ref[nq + nk :, :] = mm(selk, wv_s[...]).astype(BF)
     exits[2].start()
+    for i in range(4, 8):
+        loads[i].wait()
+        sends[i].start()
+        keeps[i - 4].start()
     selkv = pad_matrix(2 * hk)
     runs = x_ref.shape[0] // RUN
     per = runs // 2
@@ -1422,8 +1424,10 @@
     gains_ref[...] = gpart[:, own]
 
 
-def finish_kernel(out_h, tg_h, gw_h, go_h, gg_h, gu_h, gd_h, out_f, tg_f, gq_f, gk_f, gv_f, go_f, gg_f, gu_f, gd_f,
+def finish_kernel(gains_ref, out_h, tg_h, gw_h, go_h, gg_h, gu_h, gd_h, one_ref, two_ref, out_f, tg_f, gq_f, gk_f, gv_f, go_f, gg_f, gu_f, gd_f,
                   out_v, tg_v, gw_v, go_v, gg_v, gu_v, gd_v, q_v, kv_v, o_v, g_v, u_v, d_v, lsem, ssem):
+    one_ref[...] = gains_ref[0]
+    two_ref[...] = gains_ref[8]
     kw = gk_f.shape[0]
     nq = gw_h.shape[1] - 2 * kw
     pairs = [(gg_h, gg_v), (gu_h, gu_v), (gd_h, gd_v), (gw_h, gw_v), (go_h, go_v), (out_h, out_v), (tg_h, tg_v)]
@@ -1563,13 +1567,13 @@
     shapes = [(rows, d), (rows, d), (dh, dq + 2 * dk), (dq, dh), (dh, ff), (dh, ff), (ff, dh)]
     wide = [(dh, dq), (2 * dk, dh), (dq, dh), (dh, ff), (dh, ff), (ff, dh)]
     finals = [(dh, dq), (dk, dh), (dk, dh), (dq, dh), (dh, ff), (dh, ff), (ff, dh)]
-    out, tg, gq, gk, gv, go, gg, gu, gd = call(
+    g1o, g2o, out, tg, gq, gk, gv, go, gg, gu, gd = call(
         finish_kernel,
-        [(a, A) for a in (out, tg, gw, go, gg, gu, gd)],
-        [(sds((rows, d), BF), A), (sds((rows, d), BF), A)] + [(sds(shape, F32), A) for shape in finals],
+        [(gains_grad, V)] + [(a, A) for a in (out, tg, gw, go, gg, gu, gd)],
+        [(sds((dh,), F32), V), (sds((dh,), F32), V), (sds((rows, d), BF), A), (sds((rows, d), BF), A)] + [(sds(shape, F32), A) for shape in finals],
         [pltpu.VMEM(shape, BF) for shape in shapes] + [pltpu.VMEM(shape, F32) for shape in wide] + [DMA((7,)), DMA((9,))],
     )
-    return out[None], tg[None], gq, gk.T, gv.T, go, gg, gu, gd, gains_grad[0], gains_grad[8]
+    return out[None], tg[None], gq, gk.T, gv.T, go, gg, gu, gd, g1o, g2o
 
 
 def body(mesh, *args):

time: 384 us -> 383 us (level)
  no operation moved by 1% of the time
where the time goes in v4:
time: 383 us
  Pallas kernels  380 us (99%)
    pallas_call x3, Pallas kernels, call(): pl.pallas_call(kernel, out_shape=[o for o, _ in outs], in_specs=[sp for _...  380 us

profile of v4, /device:TPU:1, one launch (start us, length us, event | category | flops | bytes accessed | tf_op | source)
XLA Modules:
  0.0 382.6 jit_solution(11686925871000086105)
XLA Ops:
  0.6 1.4 fusion.g_ref
  2.0 30.4 %shard_map.257 = (bf16[1024,1536]{1,0:T(8,128)(2,1)}, bf16[1024,1536]{1,0:T(8,128)(2,1)}, bf16[1024,1536]{1,0:T(8,128)(2,1)}, bf16[1024,512]{1,0:T(8,128)(2,1)},...) custom-call(bf16[1024,1536]{1,0:T(8,128)(2,1)} %bitcast.8, ...), custom_call_target="tpu_custom_call" | custom-call | flops 60000002048 | tf_op jit(solution)/shard_map/pallas_call | solution.py:1513
  32.4 336.5 %shard_map.258 = (bf16[1024,1536]{1,0:T(8,128)(2,1)}, bf16[1024,1536]{1,0:T(8,128)(2,1)}, bf16[768,1024]{1,0:T(8,128)(2,1)}, bf16[768,1024]{1,0:T(8,128)(2,1)}, ...) custom-call(s32[1,4096]{1,0:T(1,128)} %seg_ref.1, ...), custom_call_target="tpu_custom_call" | custom-call | flops 299999985664 | tf_op jit(solution)/shard_map/pallas_call | solution.py:1513
  368.9 13.4 %shard_map.259 = (f32[768]{0:T(1024)}, f32[768]{0:T(1024)}, bf16[1024,1536]{1,0:T(8,128)(2,1)}, bf16[1024,1536]{1,0:T(8,128)(2,1)}, f32[768,384]{1,0:T(8,128)}, ...) custom-call(f32[16,768]{1,0:T(8,128)} %get-tuple-element.54.gains_re, ...), custom_call_target="tpu_custom_call" | custom-call | tf_op jit(solution)/shard_map/pallas_call | solution.py:1513
